TPU v7x, 128 devices: a whole 4x4x4 slice. The times are simulated.
128 devices in a mesh: dp: 8 (over z, core), ctx: 16 (over x, y).
Axes of the slice: x: 4, y: 4, z: 4, core: 2. Of those that a mesh axis runs over, the one named last changes fastest.
Arguments:
- tokens: bfloat16 [32768, 2048], P(('dp', 'ctx')), parts along dimension 0, may hold values from -80 to 80
- qkv_weight: bfloat16 [2048, 3072], P('ctx'), may hold values from -0.125 to 0.125
- out_weight: bfloat16 [1024, 2048], P('ctx'), may hold values from -0.1875 to 0.1875
- prior_state: float32 [64, 128, 128], P('dp'), parts along dimension 0, may hold values from -240 to 240
- expert_ids: int32 [32768, 4], P(('dp', 'ctx')), parts along dimension 0, may hold values from 0 to 15, all different within a row; in each aligned block of 256 rows (0 to 255, 256 to 511, ...) at most 96 rows name the same one
- gate_weights: float32 [32768, 4], P(('dp', 'ctx')), parts along dimension 0, may hold values from 0.1 to 1
- expert_in: bfloat16 [16, 2048, 2048], P('ctx'), may hold values from -0.125 to 0.125
- expert_out: bfloat16 [16, 1024, 2048], P('ctx'), may hold values from -0.1875 to 0.1875
Outputs:
- layer_out: bfloat16 [32768, 2048], P(('dp', 'ctx')), parts along dimension 0
There are 8 independent parts, one for each index of `dp`. A program takes and returns all parts, laid end to end along the dimension named above; an argument that names none is the same for every part. Nothing has to cross between parts.
Inputs may be any that keep to these rules, and one draw needn't show every extreme that they name: `expert_ids`: within the 256 rows of one device no expert is named more than 96 times, and in some device's rows some expert is named exactly 96 times.
All inputs are finite; a program needn't handle non-finite values.
Results may differ from a plain program's by a relative error of at most 0.006.
Values may be sent and summed in bfloat16 or wider, within the bound.
No kernel may reach another device: no remote copies, remote signals or barrier semaphores. Data moves between devices by JAX's collectives and lax.ppermute only.
A program may use at most 128 MiB of HBM per device.

v0:
```python
import jax
import jax.numpy as jnp
from jax import lax
from jax.sharding import PartitionSpec as P

HEADS = 8
HD = 128
FF = 1024


EPSILON = 1e-05


def prefix(x, axis, combine, identity):
    length, index = (lax.axis_size(axis), lax.axis_index(axis))
    everything = lax.all_gather(x.astype(jnp.bfloat16), axis)
    start = jnp.broadcast_to(jnp.asarray(identity, x.dtype), x.shape)

    def step(k, before):
        reached = k < index
        new = combine(before, everything[k].astype(x.dtype))
        return jnp.where(reached, new, before)

    return lax.fori_loop(0, length, step, start)


def rms_rows(matrix):
    return matrix * lax.rsqrt(jnp.mean(matrix * matrix, axis=-1, keepdims=True) + EPSILON)


def combine_add(earlier, later):
    return earlier + later


def shards(
    tokens, qkv_weight, out_weight, prior_state, expert_ids, gate_weights, expert_in, expert_out
):
    tok_rows = tokens.shape[0]
    model_width = tokens.shape[1]
    width_heads = HEADS * HD
    groups = lax.axis_size("ctx")
    local_experts = expert_in.shape[0]
    experts = local_experts * groups
    top_count = expert_ids.shape[1]
    capacity = 3 * tok_rows * top_count // (2 * experts)
    normed = rms_rows(tokens.astype(jnp.float32)).astype(jnp.bfloat16)
    columns = normed
    projected = jnp.dot(
        columns,
        lax.all_gather(qkv_weight, "ctx", axis=0, tiled=True),
        preferred_element_type=jnp.float32,
    )
    queries = (
        jax.nn.silu(projected[:, :width_heads]).astype(jnp.bfloat16).reshape(tok_rows, HEADS, HD)
    )
    key_rows = (
        jax.nn.silu(projected[:, width_heads : 2 * width_heads])
        .astype(jnp.bfloat16)
        .reshape(tok_rows, HEADS, HD)
    )
    value_rows = projected[:, 2 * width_heads :].astype(jnp.bfloat16).reshape(tok_rows, HEADS, HD)
    local_state = jnp.einsum(
        "thd,the->hde", key_rows, value_rows, preferred_element_type=jnp.float32
    )
    earlier_sum = prefix(local_state, "ctx", combine_add, jnp.zeros_like(local_state))
    carried = prior_state + earlier_sum
    scores = jnp.einsum("thd,shd->hts", queries, key_rows, preferred_element_type=jnp.float32)
    causal = (
        jnp.arange(tok_rows, dtype=jnp.int32)[:, None]
        >= jnp.arange(tok_rows, dtype=jnp.int32)[None, :]
    )
    scores = jnp.where(causal[None], scores, jnp.float32(0.0)).astype(jnp.bfloat16)
    inside = jnp.einsum("hts,she->the", scores, value_rows, preferred_element_type=jnp.float32)
    from_state = jnp.einsum(
        "thd,hde->the", queries.astype(jnp.float32), carried, precision=lax.Precision.HIGHEST
    )
    head_normed = rms_rows(from_state + inside).astype(jnp.bfloat16).reshape(tok_rows, width_heads)
    columns = head_normed
    attended = jnp.dot(
        columns,
        lax.all_gather(out_weight, "ctx", axis=0, tiled=True),
        preferred_element_type=jnp.float32,
    )
    hidden = (tokens.astype(jnp.float32) + attended).astype(jnp.bfloat16)
    moe_in = rms_rows(hidden.astype(jnp.float32)).astype(jnp.bfloat16)
    flat_ids = expert_ids.reshape(-1)
    onehot = (flat_ids[:, None] == jnp.arange(experts, dtype=jnp.int32)[None, :]).astype(jnp.int32)
    before = jnp.cumsum(onehot, axis=0) - onehot
    slot_index = jnp.sum(before * onehot, axis=1)
    places = flat_ids * capacity + slot_index
    repeated = jnp.repeat(moe_in, top_count, axis=0)
    outgoing = jnp.zeros((experts * capacity, model_width), jnp.bfloat16).at[places].set(repeated)
    outgoing = outgoing.reshape(experts, capacity, model_width)
    arrived = lax.all_to_all(outgoing, "ctx", split_axis=0, concat_axis=0, tiled=True)
    slot_count = arrived.shape[1]
    grouped = arrived.reshape(groups, local_experts, slot_count, model_width)
    gate_up = jnp.einsum("nxid,xdf->nxif", grouped, expert_in, preferred_element_type=jnp.float32)
    middle = (jax.nn.silu(gate_up[..., :FF]) * gate_up[..., FF:]).astype(jnp.bfloat16)
    result = jnp.einsum(
        "nxif,xfd->nxid", middle, expert_out, preferred_element_type=jnp.float32
    ).astype(jnp.bfloat16)
    finished = result.reshape(groups * local_experts, slot_count, model_width)
    returned = lax.all_to_all(finished, "ctx", split_axis=0, concat_axis=0, tiled=True).reshape(
        experts * capacity, model_width
    )
    picked = returned[places].reshape(tok_rows, top_count, model_width).astype(jnp.float32)
    combined = jnp.sum(gate_weights[:, :, None] * picked, axis=1)
    return (hidden.astype(jnp.float32) + combined).astype(jnp.bfloat16)


def solution(mesh):
    return jax.shard_map(
        shards,
        mesh=mesh,
        in_specs=(
            P(("dp", "ctx"), None),
            P("ctx", None),
            P("ctx", None),
            P("dp", None, None),
            P(("dp", "ctx"), None),
            P(("dp", "ctx"), None),
            P("ctx", None, None),
            P("ctx", None, None),
        ),
        out_specs=P(("dp", "ctx"), None),
        check_vma=False,
    )
```

profile of v0, /device:TPU:124, one launch (start us, length us, event | category | flops | bytes accessed | tf_op | source)
XLA Modules:
  0.0 479.5 jit_solution(9268005951179839358)
XLA Ops:
  7.3 1.5 fusion.12
  8.8 90.0 %all-gather.5.cloned.1.call-done = bf16[2048,3072]{1,0:T(8,128)(2,1)} async-done(((bf16[128,3072]{1,0:T(8,128)(2,1)}), bf16[2048,3072]{1,0:T(8,128)(2,1)}) %all-gather.5.cloned.1.call-update) | async-done | bytes 12582928 | tf_op jit(solution)/shard_map/all_gather | solution.py:50
  98.8 6.8 %fusion.20 = f32[256,3072]{1,0:T(8,128)S(1)} fusion(bf16[2048,3072]{1,0:T(8,128)(2,1)} %all-gather.5.cloned.1.call-done, bf16[256,2048]{1,0:T(8,128)(2,1)} %param.10, f32[256]{0:T(256)S(1)} %add_rsqrt_fusion.2), kind=kOutput, calls=%fused_computation.31 | convolution fusion | flops 3222798336 | bytes 16778240 | tf_op jit(solution)/shard_map/dot_general | solution.py:48
  108.8 4.5 reduce-window.6
  114.1 44.8 %all-gather.9.cloned.1.call-done = bf16[128,128,128]{2,1,0:T(8,128)(2,1)} async-done(((bf16[8,128,128]{2,1,0:T(8,128)(2,1)}), bf16[128,128,128]{2,1,0:T(8,128)(2,1)}) %all-gather.9.cloned.1.call-update) | async-done | bytes 4194320 | tf_op jit(solution)/shard_map/all_gather | solution.py:16
  158.9 20.1 %while.14 = (s32[]{:T(128)}, f32[8,128,128]{2,1,0:T(8,128)S(1)}, s32[]{:T(128)}, bf16[16,8,128,128]{3,2,1,0:T(8,128)(2,1)}, s32[]{:T(128)}, /*index=5*/s32[]{:T(128)}) while((s32[]{:T(128)}, f32[8,128,128]{2,1,0:T(8,128)S(1)}, s32[]{:T(128)}, bf16[16,8,128,128]{3,2,1,0:T(8,128)(2,1)}, s32[]{:T(128)}, /*index=5*/s32[]{:T(128)}) %tuple.44), condition=%wide.region_2.3_spmd.clone, body=%wide.region_1.2_spmd.clone.sunk | while | flops 524292 | bytes 1310813 | solution.py:24
  160.1 1.2 add_select_fusion.2
  161.4 1.2 add_select_fusion.2
  162.6 1.2 add_select_fusion.2
  163.9 1.2 add_select_fusion.2
  165.1 1.2 add_select_fusion.2
  166.4 1.2 add_select_fusion.2
  171.4 1.2 add_select_fusion.2
  172.7 1.3 add_select_fusion.2
  176.5 1.2 add_select_fusion.2
  177.8 1.2 add_select_fusion.2
  179.0 1.6 fusion.27
  180.6 2.0 multiply_reduce_fusion.1
  182.7 29.4 %all-gather.7.cloned.1.call-done = bf16[1024,2048]{1,0:T(8,128)(2,1)} async-done(((bf16[64,2048]{1,0:T(8,128)(2,1)}), bf16[1024,2048]{1,0:T(8,128)(2,1)}) %all-gather.7.cloned.1.call-update) | async-done | bytes 4194320 | tf_op jit(solution)/shard_map/all_gather | solution.py:81
  212.1 3.9 fusion.14
  216.3 4.1 broadcast_in_dim.35
  220.4 6.9 %reshape.150 = bf16[1024,2048]{1,0:T(8,128)(2,1)} reshape(bf16[256,4,2048]{2,1,0:T(4,128)(2,1)} %broadcast_in_dim.35) | data formatting | bytes 8388608 | tf_op jit(solution)/shard_map/reshape | solution.py:91
  227.3 11.2 %scatter_custom_fusion = bf16[1536,2048]{1,0:T(8,128)(2,1)} fusion(s32[1024]{0:T(1024)S(1)} %bitcast.85, bf16[1024,2048]{1,0:T(8,128)(2,1)} %reshape.150, bf16[]{:T(256)} %constant.55.clone.1), kind=kCustom, calls=%fused_computation.12 | custom fusion | bytes 6291968 | tf_op jit(solution)/shard_map/scatter | solution.py:92
  238.5 77.4 %all_to_all.10 = bf16[16,96,2048]{2,1,0:T(8,128)(2,1)S(1)} all-to-all(bf16[16,96,2048]{2,1,0:T(8,128)(2,1)} %bitcast.77), channel_id=1, replica_groups=mesh['dp'=8,'ctx'=16] {'ctx'}, dimensions={0} | all-to-all | bytes 12582912 | tf_op jit(solution)/shard_map/all_to_all | solution.py:94
  316.0 16.2 %fusion.3 = f32[16,1,96,2048]{3,2,0,1:T(8,128)S(1)} fusion(bf16[16,96,2048]{2,1,0:T(8,128)(2,1)S(1)} %all_to_all.10, bf16[1,2048,2048]{2,1,0:T(8,128)(2,1)} %param.16), kind=kOutput, calls=%fused_computation.8 | convolution fusion | flops 12884901888 | bytes 27262976 | tf_op jit(solution)/shard_map/nxid,xdf->nxif/dot_general | solution.py:97
  332.2 8.6 %convolution_convert_fusion = bf16[16,96,2048]{2,1,0:T(8,128)(2,1)} fusion(bf16[1,1024,2048]{2,1,0:T(8,128)(2,1)S(1)} %copy-done.3, f32[16,1,96,2048]{3,2,0,1:T(8,128)S(1)} %fusion.3), kind=kOutput, calls=%fused_computation.9 | convolution fusion | flops 6455033856 | bytes 23068672 | tf_op jit(solution)/shard_map/nxif,xfd->nxid/dot_general | solution.py:99
  340.8 8.0 %all-to-all-start.1 = ((bf16[16,96,2048]{2,1,0:T(8,128)(2,1)}), bf16[16,96,2048]{2,1,0:T(8,128)(2,1)}, u32[]{:S(2)}, u32[]{:S(2)}) async-start(bf16[16,96,2048]{2,1,0:T(8,128)(2,1)} %convolution_convert_fusion), calls=%async_computation.1 | async-start | bytes 12582912 | tf_op jit(solution)/shard_map/all_to_all | solution.py:103
  349.0 92.0 %all-to-all-done.1 = bf16[16,96,2048]{2,1,0:T(8,128)(2,1)} async-done(((bf16[16,96,2048]{2,1,0:T(8,128)(2,1)}), bf16[16,96,2048]{2,1,0:T(8,128)(2,1)}, u32[]{:S(2)}, u32[]{:S(2)}) %all-to-all-start.1) | async-done | bytes 6291488 | tf_op jit(solution)/shard_map/all_to_all | solution.py:103
  441.0 12.4 %gather_fusion = bf16[1024,2048]{1,0:T(8,128)(2,1)} fusion(bf16[1536,2048]{1,0:T(8,128)(2,1)} %bitcast.18, s32[1024]{0:T(1024)S(1)} %broadcast_clamp_fusion), kind=kCustom, calls=%fused_computation | custom fusion | bytes 8392704 | tf_op jit(solution)/shard_map/gather | solution.py:106
  453.4 8.3 %reshape.137 = f32[256,4,2048]{2,1,0:T(4,128)} reshape(bf16[1024,2048]{1,0:T(8,128)(2,1)} %gather_fusion) | data formatting | bytes 12582912 | tf_op jit(solution)/shard_map/convert_element_type | solution.py:106
  461.7 10.0 %multiply_reduce_fusion = f32[256,2048]{1,0:T(8,128)S(1)} fusion(f32[256,4,2048]{2,1,0:T(4,128)} %reshape.137, f32[256,4]{1,0:T(8,128)S(1)} %copy.35), kind=kLoop, calls=%fused_computation.5 | loop fusion | flops 3670016 | bytes 10489856 | tf_op jit(solution)/shard_map/reduce_sum | solution.py:107
  471.8 1.3 fusion.16
  (48 shorter events, 12.4 us)
Async XLA Ops:
  6.5 92.3 %all-gather.5.cloned.1.call-start = ((), (), s32[]{:S(2)}) async-start(), calls=%async_computation.2 | async-start | bytes 13369344 | tf_op jit(solution)/shard_map/all_gather | solution.py:50
  7.3 151.6 %all-gather.9.cloned.1.call-start = ((), (), s32[]{:S(2)}) async-start(), calls=%async_computation.4 | async-start | bytes 4456448 | tf_op jit(solution)/shard_map/all_gather | solution.py:16
  105.6 2.7 copy-start.1
  107.6 71.4 %copy-start = (f32[8,128,128]{2,1,0:T(8,128)S(1)}, f32[8,128,128]{2,1,0:T(8,128)}, u32[]{:S(2)}) copy-start(f32[8,128,128]{2,1,0:T(8,128)} %param.13) | copy-start | bytes 1572868
  107.6 104.5 %all-gather.7.cloned.1.call-start = ((), (), s32[]{:S(2)}) async-start(), calls=%async_computation.3 | async-start | bytes 4456448 | tf_op jit(solution)/shard_map/all_gather | solution.py:81
  316.0 16.2 %copy-start.3 = (bf16[1,1024,2048]{2,1,0:T(8,128)(2,1)S(1)}, bf16[1,1024,2048]{2,1,0:T(8,128)(2,1)}, u32[]{:S(2)}) copy-start(bf16[1,1024,2048]{2,1,0:T(8,128)(2,1)} %param.17) | copy-start | bytes 12582916
  340.8 8.0 %copy-start.2 = (f32[256,4]{0,1:T(4,128)S(1)}, f32[256,4]{0,1:T(4,128)}, u32[]{:S(2)}) copy-start(f32[256,4]{0,1:T(4,128)} %param.15) | copy-start | bytes 12292
  340.8 100.2 %all-to-all-start.1 = ((bf16[16,96,2048]{2,1,0:T(8,128)(2,1)}), bf16[16,96,2048]{2,1,0:T(8,128)(2,1)}, u32[]{:S(2)}, u32[]{:S(2)}) async-start(bf16[16,96,2048]{2,1,0:T(8,128)(2,1)} %convolution_convert_fusion), calls=%async_computation.1 | async-start | bytes 12582912 | tf_op jit(solution)/shard_map/all_to_all | solution.py:103
Sparse Core Ops, SparseCore 0:
  9.5 89.2 all-gather.4
  107.7 51.0 all-gather.8
  161.0 51.0 all-gather.6
where the time goes:
time: 482 us; the launch traced here: 480 us
  waiting for transfers between devices  258 us (54%)
  blocking collectives  77.4 us (16%)
  local copies, waits for them, and re-layouts  44.3 us (9%)
  matrix products  40.1 us (8%)
  other arithmetic  38.2 us (8%)
  between operations  13.3 us (3%)
  starting transfers between devices  8.26 us (2%)
    all_to_all x1, waiting for transfers between devices, shards(): lax.all_to_all(finished, 'ctx', split_axis=0, concat_axis=0, tiled=True)  92 us
    all_gather x1, waiting for transfers between devices, shards(): lax.all_gather(qkv_weight, 'ctx', axis=0, tiled=True)  90 us
    all_to_all x1, blocking collectives, shards(): lax.all_to_all(outgoing, 'ctx', split_axis=0, concat_axis=0, tiled=True)  77.4 us
    all_gather x1, waiting for transfers between devices, prefix(): everything = lax.all_gather(x.astype(jnp.bfloat16), axis)  44.8 us
    all_gather x1, waiting for transfers between devices, shards(): lax.all_gather(out_weight, 'ctx', axis=0, tiled=True)  29.4 us
    select_n x16, other arithmetic, step(): return jnp.where(reached, new, before)  19.8 us
    dot_general x1, matrix products, shards(): jnp.einsum('nxid,xdf->nxif', grouped, expert_in, preferred_element_type=j...  16.2 us
    gather x1, local copies, waits for them, and re-layouts, shards(): returned[places].reshape(tok_rows, top_count, model_width)  12.4 us
  transfers between devices with their start and end apart: 4, of which 4 were waited for; matrix products, arithmetic and copies ran while one was open for 6% of the time, Pallas kernels for 0%

commit v1 on v0

v1 whole, which is shorter than its diff:
```python
import jax
import jax.numpy as jnp
from jax import lax
from jax.sharding import PartitionSpec as P

HEADS = 8
HD = 128
FF = 1024
SIDE = 4
GROUP = 4
EPSILON = 1e-05


def rms_rows(matrix):
    return matrix * lax.rsqrt(jnp.mean(matrix * matrix, axis=-1, keepdims=True) + EPSILON)


def swap_with(x, mask):
    return lax.ppermute(x, "dp", [(i, i ^ mask) for i in range(lax.axis_size("dp"))])


def shift_ctx(x, dx, dy):
    pairs = [
        (a * SIDE + b, (a + dx) % SIDE * SIDE + (b + dy) % SIDE)
        for a in range(SIDE)
        for b in range(SIDE)
    ]
    return lax.ppermute(x, "ctx", pairs)


def gather_by_exchange(x, axis):
    count = lax.axis_size(axis)
    spread = jnp.broadcast_to(x[None], (count,) + x.shape)
    return lax.all_to_all(spread, axis, split_axis=0, concat_axis=0, tiled=True)


def routing(expert_ids, gate_weights, experts, capacity):
    rows = expert_ids.shape[0]
    names = jnp.arange(experts, dtype=jnp.int32)
    hit = expert_ids[:, :, None] == names
    member = jnp.any(hit, axis=1)
    gate = jnp.sum(jnp.where(hit, gate_weights[:, :, None], 0.0), axis=1)
    order = jnp.arange(rows, dtype=jnp.int32)
    earlier = (order[:, None] > order[None, :]).astype(jnp.bfloat16)
    slot = jnp.dot(earlier, member.astype(jnp.bfloat16), preferred_element_type=jnp.float32)
    slot = jnp.where(member, slot.astype(jnp.int32), -1)
    slots = jnp.arange(capacity, dtype=jnp.int32)
    taken_out = slot.T[:, None, :] == slots[None, :, None]
    taken_back = slot[:, :, None] == slots[None, None, :]
    send = taken_out.astype(jnp.bfloat16).reshape(experts * capacity, rows)
    high = gate.astype(jnp.bfloat16)
    low = (gate - high.astype(jnp.float32)).astype(jnp.bfloat16)
    zero = jnp.zeros((), jnp.bfloat16)
    weigh = lambda g: jnp.where(taken_back, g[:, :, None], zero).reshape(rows, experts * capacity)
    return send, jnp.concatenate([weigh(high), weigh(low)], axis=0)


def shards(
    tokens, qkv_weight, out_weight, prior_state, expert_ids, gate_weights, expert_in, expert_out
):
    rows, width = tokens.shape
    width_heads = HEADS * HD
    experts = lax.axis_size("ctx")
    capacity = 3 * rows * expert_ids.shape[1] // (2 * experts)
    own_heads = HEADS // GROUP
    own_width = own_heads * HD
    place = lax.axis_index("dp") % GROUP
    column = lax.axis_index("ctx") // SIDE
    row = lax.axis_index("ctx") % SIDE

    part = lambda n: lax.dynamic_slice_in_dim(
        qkv_weight, n * width_heads + place * own_width, own_width, axis=1
    )
    own_weight = jnp.concatenate([part(0), part(1), part(2)], axis=1)

    out_full = lax.all_gather(out_weight, "ctx", axis=0, tiled=True)
    normed = rms_rows(tokens.astype(jnp.float32)).astype(jnp.bfloat16)
    far = swap_with(normed, 2)
    near = swap_with(normed, 1)
    prior = [lax.dynamic_slice_in_dim(prior_state, place * own_heads, own_heads, axis=0)]
    for other in range(1, GROUP):
        theirs = lax.dynamic_slice_in_dim(prior_state, (place ^ other) * own_heads, own_heads, axis=0)
        prior.append(swap_with(theirs, other))
    prior = jnp.stack(prior)
    weight = gather_by_exchange(own_weight, "ctx").reshape(width, 3 * own_width)
    diagonal = swap_with(far, 1)
    everyone = jnp.concatenate([normed, near, far, diagonal], axis=0)
    send, weigh = routing(expert_ids, gate_weights, experts, capacity)

    projected = jnp.dot(everyone, weight, preferred_element_type=jnp.float32)
    split = lambda m: m.astype(jnp.bfloat16).reshape(GROUP, rows, own_heads, HD)
    queries = split(jax.nn.silu(projected[:, :own_width]))
    key_rows = split(jax.nn.silu(projected[:, own_width : 2 * own_width]))
    value_rows = split(projected[:, 2 * own_width :])

    state = jnp.einsum(
        "jthd,jthe->jhde", key_rows, value_rows, preferred_element_type=jnp.float32
    )
    sent = state.astype(jnp.bfloat16)
    in_row = [shift_ctx(sent, 0, d).astype(jnp.float32) for d in range(1, SIDE)]
    total = (state + in_row[0] + in_row[1] + in_row[2]).astype(jnp.bfloat16)
    across = [shift_ctx(total, d, 0).astype(jnp.float32) for d in range(1, SIDE)]
    carried = prior
    for d in range(1, SIDE):
        carried = carried + jnp.where(row >= d, in_row[d - 1], 0.0)
        carried = carried + jnp.where(column >= d, across[d - 1], 0.0)

    scores = jnp.einsum("jthd,jshd->jhts", queries, key_rows, preferred_element_type=jnp.float32)
    order = jnp.arange(rows, dtype=jnp.int32)
    scores = jnp.where(order[:, None] >= order[None, :], scores, 0.0).astype(jnp.bfloat16)
    inside = jnp.einsum("jhts,jshe->jthe", scores, value_rows, preferred_element_type=jnp.float32)
    high = carried.astype(jnp.bfloat16)
    low = (carried - high.astype(jnp.float32)).astype(jnp.bfloat16)
    from_state = jnp.einsum(
        "jthd,jhde->jthe", queries, high, preferred_element_type=jnp.float32
    ) + jnp.einsum("jthd,jhde->jthe", queries, low, preferred_element_type=jnp.float32)
    head_normed = rms_rows(from_state + inside).astype(jnp.bfloat16)
    head_normed = head_normed.reshape(GROUP, rows, own_width)

    back = [head_normed[0]] + [swap_with(head_normed[j], j) for j in range(1, GROUP)]
    back = jnp.stack(back)
    ordered = [lax.dynamic_index_in_dim(back, b ^ place, 0, keepdims=False) for b in range(GROUP)]
    attended = jnp.dot(
        jnp.concatenate(ordered, axis=1), out_full, preferred_element_type=jnp.float32
    )
    hidden = (tokens.astype(jnp.float32) + attended).astype(jnp.bfloat16)
    moe_in = rms_rows(hidden.astype(jnp.float32)).astype(jnp.bfloat16)

    outgoing = jnp.dot(send, moe_in, preferred_element_type=jnp.float32).astype(jnp.bfloat16)
    outgoing = outgoing.reshape(experts, capacity, width)
    arrived = lax.all_to_all(outgoing, "ctx", split_axis=0, concat_axis=0, tiled=True)
    grouped = arrived.reshape(experts * capacity, width)
    gate_up = jnp.dot(grouped, expert_in[0], preferred_element_type=jnp.float32)
    middle = (jax.nn.silu(gate_up[:, :FF]) * gate_up[:, FF:]).astype(jnp.bfloat16)
    result = jnp.dot(middle, expert_out[0], preferred_element_type=jnp.float32).astype(jnp.bfloat16)
    returned = lax.all_to_all(
        result.reshape(experts, capacity, width), "ctx", split_axis=0, concat_axis=0, tiled=True
    ).reshape(experts * capacity, width)
    combined = jnp.dot(weigh, returned, preferred_element_type=jnp.float32)
    return (hidden.astype(jnp.float32) + (combined[:rows] + combined[rows:])).astype(jnp.bfloat16)


def solution(mesh):
    return jax.shard_map(
        shards,
        mesh=mesh,
        in_specs=(
            P(("dp", "ctx"), None),
            P("ctx", None),
            P("ctx", None),
            P("dp", None, None),
            P(("dp", "ctx"), None),
            P(("dp", "ctx"), None),
            P("ctx", None, None),
            P("ctx", None, None),
        ),
        out_specs=P(("dp", "ctx"), None),
        check_vma=False,
    )
```

time: 482 us -> 373 us (0.77)
  waiting for transfers between devices: 258 us -> 186 us
  local copies, waits for them, and re-layouts: 44.3 us -> 6.84 us
  other arithmetic: 38.2 us -> 9.66 us
  starting transfers between devices: 8.26 us -> 23.1 us
  matrix products: 40.1 us -> 52.1 us
    all_gather x3 -> x1, waiting for transfers between devices: 164 us -> 0.02 us  [shards(): out_full = lax.all_gather(out_weight, 'ctx', axis=0, tiled=True)]
    ppermute x0 -> x15, waiting for transfers between devices: none -> 58.9 us  [the longest x9 34.6 us: swap_with(): lax.ppermute(x, 'dp', [(i, i ^ mask) for i in range(lax.axis_size('dp'))])]
    all_to_all x1 -> x2, waiting for transfers between devices: 92 us -> 127 us  [the longest x1 108 us: shards(): lax.all_to_all(result.reshape(experts, capacity, width), 'ctx', split_axi...]
    select_n x17 -> x1, other arithmetic: 19.8 us -> 0.28 us  [routing(): jnp.where(taken_back, g[:, :, None], zero).reshape(rows, experts * capacity)]
    gather x1 -> x0, local copies, waits for them, and re-layouts: 12.4 us -> none  [shards(): returned[places].reshape(tok_rows, top_count, model_width)]
    dot_general x7 -> x11, matrix products: 40.1 us -> 52.1 us  [the longest x1 15.7 us: shards(): gate_up = jnp.dot(grouped, expert_in[0], preferred_element_type=jnp.float32)]
    scatter x1 -> x0, local copies, waits for them, and re-layouts: 11.2 us -> none  [shards(): jnp.zeros((experts * capacity, model_width), jnp.bfloat16).at[places]]
    reduce_sum x2 -> x1, other arithmetic: 10 us -> 0.01 us  [routing(): gate = jnp.sum(jnp.where(hit, gate_weights[:, :, None], 0.0), axis=1)]
  transfers between devices with their start and end apart: 4 -> 18, of which waited for: 4 -> 12; matrix products, arithmetic and copies ran while one was open for 6% -> 7% of each run, Pallas kernels for 0% -> 0%
where the time goes in v1:
time: 373 us; the launch traced here: 372 us
  waiting for transfers between devices  186 us (50%)
  blocking collectives  80.6 us (22%)
  matrix products  52.1 us (14%)
  starting transfers between devices  23.1 us (6%)
  between operations  13.7 us (4%)
  other arithmetic  9.66 us (3%)
  local copies, waits for them, and re-layouts  6.84 us (2%)
    all_to_all x1, waiting for transfers between devices, shards(): lax.all_to_all(result.reshape(experts, capacity, width), 'ctx', split_axi...  108 us
    all_to_all x1, blocking collectives, shards(): lax.all_to_all(outgoing, 'ctx', split_axis=0, concat_axis=0, tiled=True)  80.6 us
    ppermute x9, waiting for transfers between devices, swap_with(): lax.ppermute(x, 'dp', [(i, i ^ mask) for i in range(lax.axis_size('dp'))])  34.6 us
    ppermute x6, waiting for transfers between devices, shift_ctx(): return lax.ppermute(x, 'ctx', pairs)  24.3 us
    all_to_all x1, waiting for transfers between devices, gather_by_exchange(): return lax.all_to_all(spread, axis, split_axis=0, concat_axis=0, tiled=True)  18.2 us
    dot_general x1, matrix products, shards(): gate_up = jnp.dot(grouped, expert_in[0], preferred_element_type=jnp.float32)  15.7 us
    dot_general x1, matrix products, shards(): jnp.dot(middle, expert_out[0], preferred_element_type=jnp.float32)  13.7 us
    all_to_all x1, starting transfers between devices, shards(): lax.all_to_all(result.reshape(experts, capacity, width), 'ctx', split_axi...  7.81 us
  transfers between devices with their start and end apart: 18, of which 12 were waited for; matrix products, arithmetic and copies ran while one was open for 7% of the time, Pallas kernels for 0%

profile of v1, /device:TPU:124, one launch (start us, length us, event | category | flops | bytes accessed | tf_op | source)
XLA Modules:
  0.0 372.2 jit_solution(13127794874098399859)
XLA Ops:
  8.2 2.1 broadcast_in_dim.77
  10.3 7.1 %all-to-all-start = ((bf16[16,128,768]{2,1,0:T(8,128)(2,1)}), bf16[16,128,768]{2,1,0:T(8,128)(2,1)}, u32[]{:S(2)}, u32[]{:S(2)}) async-start(bf16[16,128,768]{2,1,0:T(8,128)(2,1)} %broadcast_in_dim.77), calls=%async_computation | async-start | bytes 6291456 | tf_op jit(solution)/shard_map/all_to_all | solution.py:34
  18.5 23.9 %collective-permute-done.4 = bf16[256,2048]{1,0:T(8,128)(2,1)S(1)} collective-permute-done((bf16[256,2048]{1,0:T(8,128)(2,1)S(1)}, bf16[256,2048]{1,0:T(8,128)(2,1)S(1)}, u32[]{:S(2)}, u32[]{:S(2)}) %collective-permute-start.4) | collective-permute-done | bytes 1048608 | tf_op jit(solution)/shard_map/ppermute | solution.py:19
  43.4 1.8 collective-permute-done.5
  45.2 18.2 %all-to-all-done = bf16[16,128,768]{2,1,0:T(8,128)(2,1)} async-done(((bf16[16,128,768]{2,1,0:T(8,128)(2,1)}), bf16[16,128,768]{2,1,0:T(8,128)(2,1)}, u32[]{:S(2)}, u32[]{:S(2)}) %all-to-all-start) | async-done | bytes 3145760 | tf_op jit(solution)/shard_map/all_to_all | solution.py:34
  63.4 5.9 %fusion.3 = f32[1024,768]{1,0:T(8,128)S(1)} fusion(bf16[2048,768]{1,0:T(8,128)(2,1)} %bitcast.4, bf16[256,2048]{1,0:T(8,128)(2,1)} %collective-permute-done.5, bf16[256,2048]{1,0:T(8,128)(2,1)S(1)} %collective-permute-done.4, bf16[256,2048]{1,0:T(8,128)(2,1)} %copy-done.6, bf16[256,2048]{1,0:T(8,128)(2,1)S(1)} %fusion.16), kind=kOutput, calls=%fused_computation.6 | convolution fusion | flops 3238002688 | bytes 10485760 | tf_op jit(solution)/shard_map/dot_general | solution.py:90
  69.4 1.4 multiply_convert_fusion.2
  71.5 1.1 fusion.66
  72.5 2.0 collective-permute-start.7
  74.5 1.9 dynamic-slice_bitcast_fusion.4
  76.4 11.1 %collective-permute-done.6 = bf16[4,2,128,128]{3,2,1,0:T(8,128)(2,1)S(1)} collective-permute-done((bf16[4,2,128,128]{3,2,1,0:T(8,128)(2,1)}, bf16[4,2,128,128]{3,2,1,0:T(8,128)(2,1)S(1)}, u32[]{:S(2)}, u32[]{:S(2)}) %collective-permute-start.6) | collective-permute-done | bytes 262176 | tf_op jit(solution)/shard_map/ppermute | solution.py:28
  87.5 1.6 collective-permute-done.7
  89.1 8.3 %collective-permute-done.8 = bf16[4,2,128,128]{3,2,1,0:T(8,128)(2,1)} collective-permute-done((bf16[4,2,128,128]{3,2,1,0:T(8,128)(2,1)}, bf16[4,2,128,128]{3,2,1,0:T(8,128)(2,1)}, u32[]{:S(2)}, u32[]{:S(2)}) %collective-permute-start.8) | collective-permute-done | bytes 262176 | tf_op jit(solution)/shard_map/ppermute | solution.py:28
  97.4 1.9 fusion.40
  100.1 2.0 collective-permute-start.9
  103.6 5.1 %collective-permute-done.1 = f32[2,128,128]{2,1,0:T(8,128)} collective-permute-done((f32[2,128,128]{2,1,0:T(8,128)}, f32[2,128,128]{2,1,0:T(8,128)}, u32[]{:S(2)}, u32[]{:S(2)}) %collective-permute-start.1) | collective-permute-done | bytes 131104 | tf_op jit(solution)/shard_map/ppermute | solution.py:19
  110.3 1.9 collective-permute-done.9
  112.2 1.7 fusion.39
  114.2 1.3 convolution_add_fusion
  115.6 2.9 multiply_reduce_fusion
  118.5 1.3 multiply_convert_fusion
  120.4 1.7 collective-permute-start.12
  122.6 3.7 collective-permute-done.13
  126.4 3.6 fusion.17
  130.0 1.9 convolution_convert_fusion
  131.9 80.6 %all_to_all.15 = bf16[16,96,2048]{2,1,0:T(8,128)(2,1)S(1)} all-to-all(bf16[16,96,2048]{2,1,0:T(8,128)(2,1)S(1)} %bitcast.54), channel_id=1, replica_groups=mesh['dp'=8,'ctx'=16] {'ctx'}, dimensions={0} | all-to-all | bytes 12582912 | tf_op jit(solution)/shard_map/all_to_all | solution.py:131
  212.5 15.7 %fusion = f32[1536,2048]{1,0:T(8,128)} fusion(bf16[1536,2048]{1,0:T(8,128)(2,1)S(1)} %bitcast.56, bf16[1,2048,2048]{2,1,0:T(8,128)(2,1)S(1)} %bitcast.66), kind=kOutput, calls=%fused_computation | convolution fusion | flops 12884901888 | bytes 27262976 | tf_op jit(solution)/shard_map/dot_general | solution.py:133
  228.2 13.7 %convolution_convert_fusion.1 = bf16[1536,2048]{1,0:T(8,128)(2,1)} fusion(bf16[1,1024,2048]{2,1,0:T(8,128)(2,1)S(1)} %copy-done.5, f32[1536,2048]{1,0:T(8,128)} %fusion), kind=kOutput, calls=%fused_computation.3 | convolution fusion | flops 6455033856 | bytes 23068672 | tf_op jit(solution)/shard_map/dot_general | solution.py:135
  241.9 7.8 %all-to-all-start.2 = ((bf16[16,96,2048]{2,1,0:T(8,128)(2,1)}), bf16[16,96,2048]{2,1,0:T(8,128)(2,1)}, u32[]{:S(2)}, u32[]{:S(2)}) async-start(bf16[16,96,2048]{2,1,0:T(8,128)(2,1)} %bitcast.55), calls=%async_computation.2 | async-start | bytes 12582912 | tf_op jit(solution)/shard_map/all_to_all | solution.py:136
  250.0 108.4 %all-to-all-done.2 = bf16[16,96,2048]{2,1,0:T(8,128)(2,1)} async-done(((bf16[16,96,2048]{2,1,0:T(8,128)(2,1)}), bf16[16,96,2048]{2,1,0:T(8,128)(2,1)}, u32[]{:S(2)}, u32[]{:S(2)}) %all-to-all-start.2) | async-done | bytes 6291488 | tf_op jit(solution)/shard_map/all_to_all | solution.py:136
  358.4 5.5 %fusion.20 = f32[512,2048]{1,0:T(8,128)S(1)} fusion(bf16[1536,2048]{1,0:T(8,128)(2,1)} %bitcast.27, bf16[256,1536]{0,1:T(8,128)(2,1)S(1)} %get-tuple-element.25, bf16[256,1536]{0,1:T(8,128)(2,1)S(1)} %get-tuple-element.24), kind=kOutput, calls=%fused_computation.30 | convolution fusion | flops 3224371200 | bytes 12058624 | tf_op jit(solution)/shard_map/dot_general | solution.py:139
  363.9 1.5 fusion.19
  (66 shorter events, 10.2 us)
Async XLA Ops:
  6.5 119.9 %all-gather.2.cloned.1.call-start = ((), (), s32[]{:S(2)}) async-start(), calls=%async_computation.3 | async-start | bytes 4456448 | tf_op jit(solution)/shard_map/all_gather | solution.py:76
  8.2 9.2 %copy-start = (bf16[256,2048]{1,0:T(8,128)(2,1)S(1)}, bf16[256,2048]{1,0:T(8,128)(2,1)}, u32[]{:S(2)}) copy-start(bf16[256,2048]{1,0:T(8,128)(2,1)} %param.8) | copy-start | bytes 3145732
  10.3 53.1 %all-to-all-start = ((bf16[16,128,768]{2,1,0:T(8,128)(2,1)}), bf16[16,128,768]{2,1,0:T(8,128)(2,1)}, u32[]{:S(2)}, u32[]{:S(2)}) async-start(bf16[16,128,768]{2,1,0:T(8,128)(2,1)} %broadcast_in_dim.77), calls=%async_computation | async-start | bytes 6291456 | tf_op jit(solution)/shard_map/all_to_all | solution.py:34
  18.0 24.4 %collective-permute-start.4 = (bf16[256,2048]{1,0:T(8,128)(2,1)S(1)}, bf16[256,2048]{1,0:T(8,128)(2,1)S(1)}, u32[]{:S(2)}, u32[]{:S(2)}) collective-permute-start(bf16[256,2048]{1,0:T(8,128)(2,1)S(1)} %fusion.16), channel_id=1, source_target_pairs={{0,32},{16,48},{32,0},{48,16},{64,96},{80,112},{96,64},{112,80},{1... | collective-permute-start | bytes 3145736 | tf_op jit(solution)/shard_map/ppermute | solution.py:19
  18.5 23.9 %collective-permute-start.3 = (bf16[256,2048]{1,0:T(8,128)(2,1)S(1)}, bf16[256,2048]{1,0:T(8,128)(2,1)S(1)}, u32[]{:S(2)}, u32[]{:S(2)}) collective-permute-start(bf16[256,2048]{1,0:T(8,128)(2,1)S(1)} %fusion.16), channel_id=1, source_target_pairs={{0,16},{16,0},{32,48},{48,32},{64,80},{80,64},{96,112},{112,96},{1... | collective-permute-start | bytes 3145736 | tf_op jit(solution)/shard_map/ppermute | solution.py:19
  42.4 2.8 collective-permute-start.5
  42.4 1.0 copy-start.6
  70.8 31.9 %copy-start.3 = (s32[256,4]{0,1:T(4,128)S(1)}, s32[256,4]{0,1:T(4,128)}, u32[]{:S(2)}) copy-start(s32[256,4]{0,1:T(4,128)} %param.12) | copy-start | bytes 12292
  71.4 32.1 %copy-start.1 = (bf16[1024,256]{1,0:T(8,128)(2,1)S(1)}, bf16[1024,256]{1,0:T(8,128)(2,1)}, u32[]{:S(2)}) copy-start(bf16[1024,256]{1,0:T(8,128)(2,1)} %get-tuple-element.8) | copy-start | bytes 1572868
  72.5 15.0 %collective-permute-start.6 = (bf16[4,2,128,128]{3,2,1,0:T(8,128)(2,1)}, bf16[4,2,128,128]{3,2,1,0:T(8,128)(2,1)S(1)}, u32[]{:S(2)}, u32[]{:S(2)}) collective-permute-start(bf16[4,2,128,128]{3,2,1,0:T(8,128)(2,1)} %get-tuple-element.26), channel_id=1, source_target_pairs={{0,1},{1,2},{2,3},{3,0},{4,5},{5,6},{6,7},{7,4},{8,9},{9,10},{10,1... | collective-permute-start | bytes 786440 | tf_op jit(solution)/shard_map/ppermute | solution.py:28
  72.5 16.6 %collective-permute-start.7 = (bf16[4,2,128,128]{3,2,1,0:T(8,128)(2,1)}, bf16[4,2,128,128]{3,2,1,0:T(8,128)(2,1)}, u32[]{:S(2)}, u32[]{:S(2)}) collective-permute-start(bf16[4,2,128,128]{3,2,1,0:T(8,128)(2,1)} %get-tuple-element.26), channel_id=1, source_target_pairs={{0,2},{1,3},{2,0},{3,1},{4,6},{5,7},{6,4},{7,5},{8,10},{9,11},{10,... | collective-permute-start | bytes 786440 | tf_op jit(solution)/shard_map/ppermute | solution.py:28
  74.5 22.9 %collective-permute-start.8 = (bf16[4,2,128,128]{3,2,1,0:T(8,128)(2,1)}, bf16[4,2,128,128]{3,2,1,0:T(8,128)(2,1)}, u32[]{:S(2)}, u32[]{:S(2)}) collective-permute-start(bf16[4,2,128,128]{3,2,1,0:T(8,128)(2,1)} %get-tuple-element.26), channel_id=1, source_target_pairs={{0,3},{1,0},{2,1},{3,2},{4,7},{5,4},{6,5},{7,6},{8,11},{9,8},{10,9... | collective-permute-start | bytes 786440 | tf_op jit(solution)/shard_map/ppermute | solution.py:28
  76.4 26.3 %collective-permute-start = (f32[2,128,128]{2,1,0:T(8,128)S(1)}, f32[2,128,128]{2,1,0:T(8,128)}, u32[]{:S(2)}, u32[]{:S(2)}) collective-permute-start(f32[2,128,128]{2,1,0:T(8,128)S(1)} %get-tuple-element.21), channel_id=1, source_target_pairs={{0,16},{16,0},{32,48},{48,32},{64,80},{80,64},{96,112},{112,96},{1... | collective-permute-start | bytes 393224 | tf_op jit(solution)/shard_map/ppermute | solution.py:19
  99.2 10.3 %collective-permute-start.10 = (bf16[4,2,128,128]{3,2,1,0:T(8,128)(2,1)}, bf16[4,2,128,128]{3,2,1,0:T(8,128)(2,1)}, u32[]{:S(2)}, u32[]{:S(2)}) collective-permute-start(bf16[4,2,128,128]{3,2,1,0:T(8,128)(2,1)} %fusion.40), channel_id=1, source_target_pairs={{0,8},{1,9},{2,10},{3,11},{4,12},{5,13},{6,14},{7,15},{8,0},{9,1},... | collective-permute-start | bytes 786440 | tf_op jit(solution)/shard_map/ppermute | solution.py:28
  100.1 10.2 %collective-permute-start.11 = (bf16[4,2,128,128]{3,2,1,0:T(8,128)(2,1)}, bf16[4,2,128,128]{3,2,1,0:T(8,128)(2,1)}, u32[]{:S(2)}, u32[]{:S(2)}) collective-permute-start(bf16[4,2,128,128]{3,2,1,0:T(8,128)(2,1)} %fusion.40), channel_id=1, source_target_pairs={{0,12},{1,13},{2,14},{3,15},{4,0},{5,1},{6,2},{7,3},{8,4},{9,5},{1... | collective-permute-start | bytes 786440 | tf_op jit(solution)/shard_map/ppermute | solution.py:28
  100.1 12.1 %collective-permute-start.9 = (bf16[4,2,128,128]{3,2,1,0:T(8,128)(2,1)}, bf16[4,2,128,128]{3,2,1,0:T(8,128)(2,1)}, u32[]{:S(2)}, u32[]{:S(2)}) collective-permute-start(bf16[4,2,128,128]{3,2,1,0:T(8,128)(2,1)} %fusion.40), channel_id=1, source_target_pairs={{0,4},{1,5},{2,6},{3,7},{4,8},{5,9},{6,10},{7,11},{8,12},{9,13},{1... | collective-permute-start | bytes 786440 | tf_op jit(solution)/shard_map/ppermute | solution.py:28
  102.1 6.7 %collective-permute-start.1 = (f32[2,128,128]{2,1,0:T(8,128)}, f32[2,128,128]{2,1,0:T(8,128)}, u32[]{:S(2)}, u32[]{:S(2)}) collective-permute-start(f32[2,128,128]{2,1,0:T(8,128)} %get-tuple-element.23), channel_id=1, source_target_pairs={{0,32},{16,48},{32,0},{48,16},{64,96},{80,112},{96,64},{112,80},{1... | collective-permute-start | bytes 393224 | tf_op jit(solution)/shard_map/ppermute | solution.py:19
  102.7 6.1 %collective-permute-start.2 = (f32[2,128,128]{2,1,0:T(8,128)}, f32[2,128,128]{2,1,0:T(8,128)}, u32[]{:S(2)}, u32[]{:S(2)}) collective-permute-start(f32[2,128,128]{2,1,0:T(8,128)} %get-tuple-element.22), channel_id=1, source_target_pairs={{0,48},{16,32},{32,16},{48,0},{64,112},{80,96},{96,80},{112,64},{1... | collective-permute-start | bytes 393224 | tf_op jit(solution)/shard_map/ppermute | solution.py:19
  113.9 1.7 copy-start.2
  119.9 6.4 %collective-permute-start.13 = (bf16[256,256]{0,1:T(8,128)(2,1)S(1)}, bf16[256,256]{0,1:T(8,128)(2,1)S(1)}, u32[]{:S(2)}, u32[]{:S(2)}) collective-permute-start(bf16[256,256]{0,1:T(8,128)(2,1)S(1)} %bitcast.62), channel_id=1, source_target_pairs={{0,32},{16,48},{32,0},{48,16},{64,96},{80,112},{96,64},{112,80},{1... | collective-permute-start | bytes 393224 | tf_op jit(solution)/shard_map/ppermute | solution.py:19
  120.4 5.8 %collective-permute-start.14 = (bf16[256,256]{0,1:T(8,128)(2,1)S(1)}, bf16[256,256]{0,1:T(8,128)(2,1)S(1)}, u32[]{:S(2)}, u32[]{:S(2)}) collective-permute-start(bf16[256,256]{0,1:T(8,128)(2,1)S(1)} %bitcast.60), channel_id=1, source_target_pairs={{0,48},{16,32},{32,16},{48,0},{64,112},{80,96},{96,80},{112,64},{1... | collective-permute-start | bytes 393224 | tf_op jit(solution)/shard_map/ppermute | solution.py:19
  120.4 5.8 %collective-permute-start.12 = (bf16[256,256]{0,1:T(8,128)(2,1)S(1)}, bf16[256,256]{0,1:T(8,128)(2,1)S(1)}, u32[]{:S(2)}, u32[]{:S(2)}) collective-permute-start(bf16[256,256]{0,1:T(8,128)(2,1)S(1)} %bitcast.58), channel_id=1, source_target_pairs={{0,16},{16,0},{32,48},{48,32},{64,80},{80,64},{96,112},{112,96},{1... | collective-permute-start | bytes 393224 | tf_op jit(solution)/shard_map/ppermute | solution.py:19
  130.0 82.5 %slice-start = ((s8[8388608]{0:T(1024)(128)(4,1)}), s8[4194304]{0:T(1024)(128)(4,1)S(1)}, s32[]{:S(2)}) async-start(s8[8388608]{0:T(1024)(128)(4,1)} %bitcast.65), calls=%async_computation.4 | async-start | bytes 8388608
  131.9 80.6 %slice-start.1 = ((s8[8388608]{0:T(1024)(128)(4,1)}), s8[4194304]{0:T(1024)(128)(4,1)S(1)}, s32[]{:S(2)}) async-start(s8[8388608]{0:T(1024)(128)(4,1)} %bitcast.65), calls=%async_computation.5 | async-start | bytes 8388608
  212.5 15.7 %copy-start.5 = (bf16[1,1024,2048]{2,1,0:T(8,128)(2,1)S(1)}, bf16[1,1024,2048]{2,1,0:T(8,128)(2,1)}, u32[]{:S(2)}) copy-start(bf16[1,1024,2048]{2,1,0:T(8,128)(2,1)} %param.15) | copy-start | bytes 12582916
  241.9 7.8 %copy-start.4 = (f32[256,4]{0,1:T(4,128)S(1)}, f32[256,4]{0,1:T(4,128)}, u32[]{:S(2)}) copy-start(f32[256,4]{0,1:T(4,128)} %param.13) | copy-start | bytes 12292
  241.9 116.5 %all-to-all-start.2 = ((bf16[16,96,2048]{2,1,0:T(8,128)(2,1)}), bf16[16,96,2048]{2,1,0:T(8,128)(2,1)}, u32[]{:S(2)}, u32[]{:S(2)}) async-start(bf16[16,96,2048]{2,1,0:T(8,128)(2,1)} %bitcast.55), calls=%async_computation.2 | async-start | bytes 12582912 | tf_op jit(solution)/shard_map/all_to_all | solution.py:136
Sparse Core Ops, SparseCore 0:
  9.5 89.8 all-gather.1

commit v2 on v1

v2 whole, which is shorter than its diff:
```python
import jax
import jax.numpy as jnp
from jax import lax
from jax.experimental import pallas as pl
from jax.experimental.pallas import tpu as pltpu
from jax.sharding import PartitionSpec as P

HEADS = 8
HD = 128
FF = 1024
SIDE = 4
GROUP = 4
ROW_TILE = 512
VMEM_LIMIT = 36 << 20
EPSILON = 1e-05


def rms_rows(matrix):
    return matrix * lax.rsqrt(jnp.mean(matrix * matrix, axis=-1, keepdims=True) + EPSILON)


def swap_with(x, mask):
    return lax.ppermute(x, "dp", [(i, i ^ mask) for i in range(lax.axis_size("dp"))])


def shift_ctx(x, dx, dy):
    pairs = [
        (a * SIDE + b, (a + dx) % SIDE * SIDE + (b + dy) % SIDE)
        for a in range(SIDE)
        for b in range(SIDE)
    ]
    return lax.ppermute(x, "ctx", pairs)


def routing(expert_ids, gate_weights, experts, capacity):
    rows = expert_ids.shape[0]
    names = jnp.arange(experts, dtype=jnp.int32)
    hit = expert_ids[:, :, None] == names
    member = jnp.any(hit, axis=1)
    gate = jnp.sum(jnp.where(hit, gate_weights[:, :, None], 0.0), axis=1)
    order = jnp.arange(rows, dtype=jnp.int32)
    earlier = (order[:, None] > order[None, :]).astype(jnp.bfloat16)
    slot = jnp.dot(earlier, member.astype(jnp.bfloat16), preferred_element_type=jnp.float32)
    slot = jnp.where(member, slot.astype(jnp.int32), -1)
    slots = jnp.arange(capacity, dtype=jnp.int32)
    taken_out = slot.T[:, None, :] == slots[None, :, None]
    taken_back = slot[:, :, None] == slots[None, None, :]
    send = taken_out.astype(jnp.bfloat16).reshape(experts * capacity, rows)
    high = gate.astype(jnp.bfloat16)
    low = (gate - high.astype(jnp.float32)).astype(jnp.bfloat16)
    zero = jnp.zeros((), jnp.bfloat16)
    weigh = lambda g: jnp.where(taken_back, g[:, :, None], zero).reshape(rows, experts * capacity)
    return send, jnp.concatenate([weigh(high), weigh(low)], axis=0)


def dot32(a, b):
    return jnp.dot(a, b, preferred_element_type=jnp.float32)


def whole(a):
    return pl.BlockSpec(a.shape, lambda i: (0,) * a.ndim)


def one_of(a):
    return pl.BlockSpec((1,) + a.shape[1:], lambda i: (i,) + (0,) * (a.ndim - 1))


def call(kernel, name, grid, inputs, in_specs, outputs, out_specs, flops, scratch=()):
    size = lambda a: a.size * a.dtype.itemsize
    return pl.pallas_call(
        kernel,
        grid=(grid,),
        in_specs=in_specs,
        out_specs=out_specs,
        out_shape=outputs,
        scratch_shapes=list(scratch),
        compiler_params=pltpu.CompilerParams(vmem_limit_bytes=VMEM_LIMIT),
        cost_estimate=pl.CostEstimate(
            flops=flops,
            bytes_accessed=sum(size(a) for a in inputs) + sum(size(a) for a in outputs),
            transcendentals=0,
        ),
        name=name,
    )(*inputs)


def out_like(shape, dtype):
    return jax.ShapeDtypeStruct(shape, dtype)


def key_value_kernel(w_ref, *refs):
    rows_refs, (pair_ref, state_ref, sent_ref) = refs[:GROUP], refs[GROUP:]
    own_width = w_ref.shape[1] // 2
    for j, x_ref in enumerate(rows_refs):

        @pl.when(pl.program_id(0) == j)
        def _(x_ref=x_ref):
            both = dot32(x_ref[...], w_ref[...])
            keys = jax.nn.silu(both[:, :own_width]).astype(jnp.bfloat16)
            values = both[:, own_width:].astype(jnp.bfloat16)
            pair_ref[0, :, :own_width] = keys
            pair_ref[0, :, own_width:] = values
            for h in range(own_width // HD):
                cut = slice(h * HD, (h + 1) * HD)
                state = lax.dot_general(
                    keys[:, cut],
                    values[:, cut],
                    (((0,), (0,)), ((), ())),
                    preferred_element_type=jnp.float32,
                )
                state_ref[0, h] = state
                sent_ref[0, h] = state.astype(jnp.bfloat16)


def keys_values_states(weight, everyone):
    rows, width = everyone[0].shape
    columns = weight.shape[1]
    heads = columns // 2 // HD
    pair = out_like((GROUP, rows, columns), jnp.bfloat16)
    state = out_like((GROUP, heads, HD, HD), jnp.float32)
    sent = out_like((GROUP, heads, HD, HD), jnp.bfloat16)
    inputs = [weight, *everyone]
    outputs = [pair, state, sent]
    flops = 2 * GROUP * rows * width * columns
    return call(
        key_value_kernel, "keys_values_states", GROUP, inputs, [whole(a) for a in inputs],
        outputs, [one_of(a) for a in outputs], flops,
    )


def query_kernel(w_ref, pair_ref, *refs):
    rows_refs, (query_ref, inside_ref) = refs[:GROUP], refs[GROUP:]
    own_width = w_ref.shape[1]
    rows = pair_ref.shape[1]
    for j, x_ref in enumerate(rows_refs):

        @pl.when(pl.program_id(0) == j)
        def _(x_ref=x_ref):
            query_ref[0] = jax.nn.silu(dot32(x_ref[...], w_ref[...])).astype(jnp.bfloat16)

    causal = lax.broadcasted_iota(jnp.int32, (rows, rows), 0) >= lax.broadcasted_iota(
        jnp.int32, (rows, rows), 1
    )
    for h in range(own_width // HD):
        keys = pair_ref[0, :, h * HD : (h + 1) * HD]
        values = pair_ref[0, :, own_width + h * HD : own_width + (h + 1) * HD]
        scores = lax.dot_general(
            query_ref[0, :, h * HD : (h + 1) * HD],
            keys,
            (((1,), (1,)), ((), ())),
            preferred_element_type=jnp.float32,
        )
        scores = jnp.where(causal, scores, 0.0).astype(jnp.bfloat16)
        inside_ref[0, :, h * HD : (h + 1) * HD] = dot32(scores, values)


def queries_inside(weight, pair, everyone):
    rows, width = everyone[0].shape
    own_width = weight.shape[1]
    inputs = [weight, pair, *everyone]
    outputs = [
        out_like((GROUP, rows, own_width), jnp.bfloat16),
        out_like((GROUP, rows, own_width), jnp.float32),
    ]
    flops = 2 * GROUP * rows * own_width * (width + 2 * rows)
    return call(
        query_kernel, "queries_inside", GROUP, inputs,
        [whole(weight), one_of(pair)] + [whole(a) for a in everyone],
        outputs, [one_of(a) for a in outputs], flops,
    )


def finish_kernel(where_ref, query_ref, inside_ref, base_ref, *refs):
    across, out_ref = refs[:-1], refs[-1]
    for h in range(base_ref.shape[1]):
        carried = base_ref[0, h]
        for d, ref in enumerate(across):
            reached = (where_ref[0] > d).astype(jnp.float32)
            carried = carried + ref[0, h].astype(jnp.float32) * reached
        high = carried.astype(jnp.bfloat16)
        low = (carried - high.astype(jnp.float32)).astype(jnp.bfloat16)
        cut = slice(h * HD, (h + 1) * HD)
        query = query_ref[0, :, cut]
        mixed = dot32(query, high) + dot32(query, low) + inside_ref[0, :, cut]
        out_ref[0, :, cut] = rms_rows(mixed).astype(jnp.bfloat16)


def finished_heads(column, query, inside, base, across):
    inputs = [column.reshape(1), query, inside, base, *across]
    specs = [pl.BlockSpec(memory_space=pltpu.SMEM)] + [one_of(a) for a in inputs[1:]]
    output = out_like(query.shape, jnp.bfloat16)
    return call(
        finish_kernel, "finished_heads", GROUP, inputs, specs, [output], [one_of(output)],
        4 * query.size * HD,
    )[0]


def project_kernel(where_ref, tokens_ref, send_ref, *refs):
    back, quarters = refs[:GROUP], refs[GROUP : 2 * GROUP]
    hidden_ref, rows_ref, ordered_ref, sum_ref, normed_ref = refs[2 * GROUP :]
    own_width = back[0].shape[1]
    count, twice, narrow = quarters[0].shape
    half = twice // 2

    @pl.when(pl.program_id(0) == 0)
    def _():
        for j, ref in enumerate(back):
            at = pl.multiple_of((where_ref[0] ^ j) * own_width, own_width)
            ordered_ref[:, pl.ds(at, own_width)] = ref[...]
        heads = ordered_ref[...]
        for j, ref in enumerate(quarters):
            for n in range(2):
                weight = ref[:, n * half : (n + 1) * half, :].reshape(count * half, narrow)
                at = pl.multiple_of(((where_ref[0] ^ j) * 2 + n) * narrow, narrow)
                sum_ref[:, pl.ds(at, narrow)] = dot32(heads, weight)
        hidden = (tokens_ref[...].astype(jnp.float32) + sum_ref[...]).astype(jnp.bfloat16)
        hidden_ref[...] = hidden
        normed_ref[...] = rms_rows(hidden.astype(jnp.float32)).astype(jnp.bfloat16)

    rows_ref[...] = dot32(send_ref[...], normed_ref[...]).astype(jnp.bfloat16)


def projected_rows(place, tokens, send, back, quarters):
    rows, width = tokens.shape
    slots = send.shape[0]
    tile = slots // 4
    inputs = [place.reshape(1), tokens, send, *back, *quarters]
    specs = [pl.BlockSpec(memory_space=pltpu.SMEM), whole(tokens)]
    specs += [pl.BlockSpec((tile, rows), lambda i: (i, 0))]
    specs += [whole(a) for a in inputs[3:]]
    outputs = [out_like((rows, width), jnp.bfloat16), out_like((slots, width), jnp.bfloat16)]
    out_specs = [whole(outputs[0]), pl.BlockSpec((tile, width), lambda i: (i, 0))]
    scratch = [
        pltpu.VMEM((rows, GROUP * back[0].shape[1]), jnp.bfloat16),
        pltpu.VMEM((rows, width), jnp.float32),
        pltpu.VMEM((rows, width), jnp.bfloat16),
    ]
    flops = 2 * rows * width * (slots + GROUP * back[0].shape[1])
    return call(project_kernel, "projected_rows", 4, inputs, specs, outputs, out_specs, flops, scratch)


def expert_kernel(rows_ref, gate_ref, up_ref, out_weight_ref, out_ref, middle_ref):
    step = pl.program_id(0)
    inner = gate_ref.shape[1]
    chunks = FF // inner
    tile = ROW_TILE
    tiles = rows_ref.shape[0] // tile

    @pl.when(step < chunks)
    def _():
        at = pl.multiple_of(step * inner, inner)
        for r in range(tiles):
            cut = slice(r * tile, (r + 1) * tile)
            gate = dot32(rows_ref[cut, :], gate_ref[...])
            up = dot32(rows_ref[cut, :], up_ref[...])
            middle_ref[cut, pl.ds(at, inner)] = (jax.nn.silu(gate) * up).astype(jnp.bfloat16)

    @pl.when(step >= chunks)
    def _():
        for r in range(tiles):
            cut = slice(r * tile, (r + 1) * tile)
            out_ref[cut, :] = dot32(middle_ref[cut, :], out_weight_ref[...]).astype(jnp.bfloat16)


def expert_rows(rows, inner_weight, outer_weight):
    count, width = rows.shape
    chunks, inner, outer = FF // 256, 256, 512
    last = chunks - 1
    inputs = [rows, inner_weight, inner_weight, outer_weight]
    output = out_like((count, width), jnp.bfloat16)
    specs = [
        whole(rows),
        pl.BlockSpec((width, inner), lambda i: (0, jnp.minimum(i, last))),
        pl.BlockSpec((width, inner), lambda i: (0, chunks + jnp.minimum(i, last))),
        pl.BlockSpec((FF, outer), lambda i: (0, jnp.maximum(i - chunks, 0))),
    ]
    out_spec = pl.BlockSpec((count, outer), lambda i: (0, jnp.maximum(i - chunks, 0)))
    return call(
        expert_kernel, "expert_rows", chunks + width // outer, inputs, specs, [output], [out_spec],
        2 * count * width * 3 * FF, [pltpu.VMEM((count, FF), jnp.bfloat16)],
    )[0]


def shards(
    tokens, qkv_weight, out_weight, prior_state, expert_ids, gate_weights, expert_in, expert_out
):
    rows, width = tokens.shape
    width_heads = HEADS * HD
    experts = lax.axis_size("ctx")
    capacity = 3 * rows * expert_ids.shape[1] // (2 * experts)
    own_heads = HEADS // GROUP
    own_width = own_heads * HD
    place = lax.axis_index("dp") % GROUP
    column = lax.axis_index("ctx") // SIDE
    row = lax.axis_index("ctx") % SIDE
    cut = lambda a, start, size, axis: lax.dynamic_slice_in_dim(a, start, size, axis=axis)
    shard_rows = qkv_weight.shape[0]

    part = lambda n: cut(qkv_weight, n * width_heads + place * own_width, own_width, 1)
    first = jnp.concatenate([part(1), part(2)], axis=1)
    out_part = cut(out_weight, place * (width // GROUP), width // GROUP, 1)
    out_parts = jnp.split(out_part, width // GROUP // own_width, axis=1)
    second = jnp.concatenate([part(0)] + out_parts, axis=0)
    second = lax.all_gather(second[None], "ctx", axis=0, tiled=True)

    spread = jnp.broadcast_to(first[None], (experts,) + first.shape)
    spread, tokens = lax.optimization_barrier((spread, tokens))
    normed = rms_rows(tokens.astype(jnp.float32)).astype(jnp.bfloat16)
    far = swap_with(normed, 2)
    near = swap_with(normed, 1)
    first = lax.all_to_all(spread, "ctx", split_axis=0, concat_axis=0, tiled=True)
    everyone = [normed, near, far, swap_with(far, 1)]
    prior = [cut(prior_state, place * own_heads, own_heads, 0)]
    for other in range(1, GROUP):
        prior.append(swap_with(cut(prior_state, (place ^ other) * own_heads, own_heads, 0), other))
    first, prior = lax.optimization_barrier((first, tuple(prior)))
    prior = jnp.stack(prior)

    pair, state, sent = keys_values_states(first.reshape(width, 2 * own_width), everyone)
    in_row = [shift_ctx(sent, 0, d).astype(jnp.float32) for d in range(1, SIDE)]
    total = (state + in_row[0] + in_row[1] + in_row[2]).astype(jnp.bfloat16)
    base = prior
    for d in range(1, SIDE):
        base = base + jnp.where(row >= d, in_row[d - 1], 0.0)

    second, total = lax.optimization_barrier((second, total))
    across = [shift_ctx(total, d, 0) for d in range(1, SIDE)]
    query, inside = queries_inside(second[:, :shard_rows].reshape(width, own_width), pair, everyone)
    quarter = second[:, shard_rows:]
    quarter_far = swap_with(quarter, 2)
    quarter_near = swap_with(quarter, 1)
    send, weigh = routing(expert_ids, gate_weights, experts, capacity)

    head_normed = finished_heads(column, query, inside, base, across)
    quarter_far, head_normed = lax.optimization_barrier((quarter_far, head_normed))
    quarters = [quarter, quarter_near, quarter_far, swap_with(quarter_far, 1)]
    back = [head_normed[0]] + [swap_with(head_normed[j], j) for j in range(1, GROUP)]
    hidden, outgoing = projected_rows(place, tokens, send, back, quarters)

    outgoing, weigh, hidden = lax.optimization_barrier((outgoing, weigh, hidden))
    outgoing = outgoing.reshape(experts, capacity, width)
    arrived = lax.all_to_all(outgoing, "ctx", split_axis=0, concat_axis=0, tiled=True)
    grouped = arrived.reshape(experts * capacity, width)
    result = expert_rows(grouped, expert_in[0], expert_out[0])
    result, weigh, hidden = lax.optimization_barrier((result, weigh, hidden))
    returned = lax.all_to_all(
        result.reshape(experts, capacity, width), "ctx", split_axis=0, concat_axis=0, tiled=True
    ).reshape(experts * capacity, width)
    combined = jnp.dot(weigh, returned, preferred_element_type=jnp.float32)
    return (hidden.astype(jnp.float32) + (combined[:rows] + combined[rows:])).astype(jnp.bfloat16)


def solution(mesh):
    return jax.shard_map(
        shards,
        mesh=mesh,
        in_specs=(
            P(("dp", "ctx"), None),
            P("ctx", None),
            P("ctx", None),
            P("dp", None, None),
            P(("dp", "ctx"), None),
            P(("dp", "ctx"), None),
            P("ctx", None, None),
            P("ctx", None, None),
        ),
        out_specs=P(("dp", "ctx"), None),
        check_vma=False,
    )
```

time: 373 us -> 315 us (0.84); the launches traced: 372 us -> 310 us
  waiting for transfers between devices: 186 us -> 57.4 us
  blocking collectives: 80.6 us -> 152 us
  matrix products: 52.1 us -> 3.74 us
  Pallas kernels: 0 us -> 43.7 us
  local copies, waits for them, and re-layouts: 6.84 us -> 13.2 us
  other arithmetic: 9.66 us -> 5.79 us
    all_to_all x2 -> x1, waiting for transfers between devices: 127 us -> 0.7 us  [shards(): lax.all_to_all(spread, 'ctx', split_axis=0, concat_axis=0, tiled=True)]
    all_to_all x0 -> x1, blocking collectives: none -> 76 us  [shards(): lax.all_to_all(result.reshape(experts, capacity, width), 'ctx', split_axi...]
    dot_general x9 -> x0, matrix products: 46.5 us -> none  [the longest x1 15.7 us: shards(): gate_up = jnp.dot(grouped, expert_in[0], preferred_element_type=jnp.float32)]
    pallas_call x0 -> x5, Pallas kernels: none -> 43.7 us  [call(): pl.pallas_call(kernel, grid=(grid,), in_specs=in_specs, out_specs=out_spe...]
    all_to_all x2 -> x1, starting transfers between devices: 14.9 us -> 7.11 us  [shards(): lax.all_to_all(spread, 'ctx', split_axis=0, concat_axis=0, tiled=True)]
    all_to_all x1, blocking collectives: 80.6 us -> 75.9 us  [shards(): lax.all_to_all(outgoing, 'ctx', split_axis=0, concat_axis=0, tiled=True)]
    unnamed x18 -> x24, local copies, waits for them, and re-layouts: 1.01 us -> 5.54 us
    convert_element_type x3 -> x1, other arithmetic: 4.55 us -> 0.27 us  [routing(): send = taken_out.astype(jnp.bfloat16).reshape(experts * capacity, rows)]
  transfers between devices with their start and end apart: 18 -> 20, of which waited for: 12 -> 12; matrix products, arithmetic and copies ran while one was open for 7% -> 2% of each run, Pallas kernels for 0% -> 5%
where the time goes in v2:
time: 315 us; the launch traced here: 310 us
  blocking collectives  152 us (48%)
  waiting for transfers between devices  57.4 us (18%)
  Pallas kernels  43.7 us (14%)
  starting transfers between devices  20.6 us (7%)
  between operations  13.6 us (4%)
  local copies, waits for them, and re-layouts  13.2 us (4%)
  other arithmetic  5.79 us (2%)
  matrix products  3.74 us (1%)
    all_to_all x1, blocking collectives, shards(): lax.all_to_all(result.reshape(experts, capacity, width), 'ctx', split_axi...  76 us
    all_to_all x1, blocking collectives, shards(): lax.all_to_all(outgoing, 'ctx', split_axis=0, concat_axis=0, tiled=True)  75.9 us
    pallas_call x5, Pallas kernels, call(): pl.pallas_call(kernel, grid=(grid,), in_specs=in_specs, out_specs=out_spe...  43.7 us
    ppermute x12, waiting for transfers between devices, swap_with(): lax.ppermute(x, 'dp', [(i, i ^ mask) for i in range(lax.axis_size('dp'))])  34.6 us
    ppermute x6, waiting for transfers between devices, shift_ctx(): return lax.ppermute(x, 'ctx', pairs)  22 us
    ppermute x6, starting transfers between devices, shift_ctx(): return lax.ppermute(x, 'ctx', pairs)  8.11 us
    all_to_all x1, starting transfers between devices, shards(): lax.all_to_all(spread, 'ctx', split_axis=0, concat_axis=0, tiled=True)  7.11 us
  transfers between devices with their start and end apart: 20, of which 12 were waited for; matrix products, arithmetic and copies ran while one was open for 2% of the time, Pallas kernels for 5%

profile of v2, /device:TPU:124, one launch (start us, length us, event | category | flops | bytes accessed | tf_op | source)
XLA Modules:
  0.0 310.1 jit_solution(4946098304108086536)
XLA Ops:
  9.0 1.6 broadcast_in_dim.65
  11.6 7.1 %all-to-all-start = ((bf16[16,128,512]{2,1,0:T(8,128)(2,1)}), bf16[16,128,512]{2,1,0:T(8,128)(2,1)}, u32[]{:S(2)}, u32[]{:S(2)}) async-start(bf16[16,128,512]{2,1,0:T(8,128)(2,1)} %broadcast_in_dim.65), calls=%async_computation | async-start | bytes 4194304 | tf_op jit(solution)/shard_map/all_to_all | solution.py:311
  18.8 17.4 %collective-permute-done.4.refs_2_ = bf16[256,2048]{1,0:T(8,128)(2,1)S(1)} collective-permute-done((bf16[256,2048]{1,0:T(8,128)(2,1)S(1)}, bf16[256,2048]{1,0:T(8,128)(2,1)S(1)}, u32[]{:S(2)}, u32[]{:S(2)}) %collective-permute-start.4) | collective-permute-done | bytes 1048608 | tf_op jit(solution)/shard_map/ppermute | solution.py:23
  36.1 1.5 constant_dynamic-slice_fusion.1
  38.3 1.6 collective-permute-start.1
  39.9 3.3 %collective-permute-done.2 = f32[2,128,128]{2,1,0:T(8,128)S(1)} collective-permute-done((f32[2,128,128]{2,1,0:T(8,128)S(1)}, f32[2,128,128]{2,1,0:T(8,128)S(1)}, u32[]{:S(2)}, u32[]{:S(2)}) %collective-permute-start.2) | collective-permute-done | bytes 131104 | tf_op jit(solution)/shard_map/ppermute | solution.py:23
  44.5 1.9 collective-permute-done.1
  47.2 6.0 %keys_values_states.1 = (bf16[4,256,512]{2,1,0:T(8,128)(2,1)S(1)}, f32[4,2,128,128]{3,2,1,0:T(8,128)S(1)}, bf16[4,2,128,128]{3,2,1,0:T(8,128)(2,1)S(1)}) custom-call(bf16[2048,512]{1,0:T(8,128)(2,1)} %bitcast.4.w_ref, bf16[256,2048]{1,0:T(8,128)(2,1)S(1)} %fusion.1.refs_0_, bf16[256,2048]{1,0:T(8,128)(2,1)} %collective-permute-done.3.refs_1_, ...), custom_call_target="tpu_custom_call" | custom-call | flops 2147483648 | bytes 8126464 | tf_op jit(solution)/shard_map/keys_values_states/pallas_call | solution.py:70
  55.0 1.2 collective-permute-start.8
  56.1 2.5 collective-permute-start.7
  58.7 1.2 collective-permute-start.6
  59.8 10.8 %collective-permute-done.8 = bf16[4,2,128,128]{3,2,1,0:T(8,128)(2,1)S(1)} collective-permute-done((bf16[4,2,128,128]{3,2,1,0:T(8,128)(2,1)S(1)}, bf16[4,2,128,128]{3,2,1,0:T(8,128)(2,1)S(1)}, u32[]{:S(2)}, u32[]{:S(2)}) %collective-permute-start.8) | collective-permute-done | bytes 262176 | tf_op jit(solution)/shard_map/ppermute | solution.py:32
  70.6 4.1 %collective-permute-done.7 = bf16[4,2,128,128]{3,2,1,0:T(8,128)(2,1)S(1)} collective-permute-done((bf16[4,2,128,128]{3,2,1,0:T(8,128)(2,1)S(1)}, bf16[4,2,128,128]{3,2,1,0:T(8,128)(2,1)S(1)}, u32[]{:S(2)}, u32[]{:S(2)}) %collective-permute-start.7) | collective-permute-done | bytes 262176 | tf_op jit(solution)/shard_map/ppermute | solution.py:32
  74.7 3.4 %collective-permute-done.6 = bf16[4,2,128,128]{3,2,1,0:T(8,128)(2,1)S(1)} collective-permute-done((bf16[4,2,128,128]{3,2,1,0:T(8,128)(2,1)S(1)}, bf16[4,2,128,128]{3,2,1,0:T(8,128)(2,1)S(1)}, u32[]{:S(2)}, u32[]{:S(2)}) %collective-permute-start.6) | collective-permute-done | bytes 262176 | tf_op jit(solution)/shard_map/ppermute | solution.py:32
  78.1 2.3 fusion.10
  80.5 2.7 fusion.13
  84.5 2.4 collective-permute-start.11
  87.1 1.2 copy-done.3
  88.3 1.2 copy-done.5
  89.5 5.5 %queries_inside.1 = (bf16[4,256,256]{2,1,0:T(8,128)(2,1)S(1)}, f32[4,256,256]{2,1,0:T(8,128)S(1)}) custom-call(bf16[2048,256]{1,0:T(8,128)(2,1)S(1)} %bitcast.44, bf16[4,256,512]{2,1,0:T(8,128)(2,1)S(1)} %copy-done.5, bf16[256,2048]{1,0:T(8,128)(2,1)S(1)} %fusion.1.refs_0_, bf16[256,2048]{1,0:T(8,128)(2,1)} %collective-permute-done.3.refs_1_, ...), custom_call_target="tpu_custom_call" | custom-call | flops 1342177280 | bytes 7864320 | tf_op jit(solution)/shard_map/queries_inside/pallas_call | solution.py:70
  95.6 3.2 %collective-permute-done.10.refs_0_ = bf16[4,2,128,128]{3,2,1,0:T(8,128)(2,1)} collective-permute-done((bf16[4,2,128,128]{3,2,1,0:T(8,128)(2,1)}, bf16[4,2,128,128]{3,2,1,0:T(8,128)(2,1)}, u32[]{:S(2)}, u32[]{:S(2)}) %collective-permute-start.10) | collective-permute-done | bytes 262176 | tf_op jit(solution)/shard_map/ppermute | solution.py:32
  98.8 2.9 finished_heads.1
  101.8 5.9 %collective-permute-done.9.refs_6_ = bf16[16,128,256]{2,1,0:T(8,128)(2,1)} collective-permute-done((bf16[16,128,256]{2,1,0:T(8,128)(2,1)}, bf16[16,128,256]{2,1,0:T(8,128)(2,1)}, u32[]{:S(2)}, u32[]{:S(2)}) %collective-permute-start.9) | collective-permute-done | bytes 1048608 | tf_op jit(solution)/shard_map/ppermute | solution.py:23
  108.7 1.7 collective-permute-start.14
  110.8 2.6 collective-permute-done.15.refs_3_
  113.4 3.5 %collective-permute-done.14.refs_2_ = bf16[256,256]{1,0:T(8,128)(2,1)S(1)} collective-permute-done((bf16[256,256]{1,0:T(8,128)(2,1)S(1)}, bf16[256,256]{1,0:T(8,128)(2,1)S(1)}, u32[]{:S(2)}, u32[]{:S(2)}) %collective-permute-start.14) | collective-permute-done | bytes 131104 | tf_op jit(solution)/shard_map/ppermute | solution.py:23
  116.9 5.7 %projected_rows.1 = (bf16[256,2048]{1,0:T(8,128)(2,1)S(1)}, bf16[1536,2048]{1,0:T(8,128)(2,1)S(1)}) custom-call(s32[1]{0:T(128)} %bitcast.where_ref, bf16[256,2048]{1,0:T(8,128)(2,1)S(1)} %copy-done, bf16[1536,256]{1,0:T(8,128)(2,1)S(1)} %fusion.6.send_ref, bf16[256,256]{1,0:T(8,128)(2,1)S(1)} %get-tuple-element.65.refs_0_, ...), custom_call_target="tpu_custom_call" | custom-call | flops 2684354560 | bytes 13893636 | tf_op jit(solution)/shard_map/projected_rows/pallas_call | solution.py:70
  122.6 75.9 %all_to_all.15 = bf16[16,96,2048]{2,1,0:T(8,128)(2,1)S(1)} all-to-all(bf16[16,96,2048]{2,1,0:T(8,128)(2,1)S(1)} %bitcast.41), channel_id=1, replica_groups=mesh['dp'=8,'ctx'=16] {'ctx'}, dimensions={0} | all-to-all | bytes 12582912 | tf_op jit(solution)/shard_map/all_to_all | solution.py:342
  198.6 23.5 %expert_rows.1 = bf16[1536,2048]{1,0:T(8,128)(2,1)S(1)} custom-call(bf16[1536,2048]{1,0:T(8,128)(2,1)S(1)} %bitcast.42, bf16[2048,2048]{1,0:T(8,128)(2,1)} %bitcast.52, bf16[2048,2048]{1,0:T(8,128)(2,1)} %bitcast.53, bf16[1024,2048]{1,0:T(8,128)(2,1)S(1)} %bitcast.45), custom_call_target="tpu_custom_call" | custom-call | flops 19327352832 | bytes 33554432 | tf_op jit(solution)/shard_map/expert_rows/pallas_call | solution.py:70
  222.1 76.0 %all_to_all.16 = bf16[16,96,2048]{2,1,0:T(8,128)(2,1)S(1)} all-to-all(bf16[16,96,2048]{2,1,0:T(8,128)(2,1)S(1)} %bitcast.43), channel_id=1, replica_groups=mesh['dp'=8,'ctx'=16] {'ctx'}, dimensions={0} | all-to-all | bytes 12582912 | tf_op jit(solution)/shard_map/all_to_all | solution.py:346
  298.1 3.6 %fusion.14 = f32[512,2048]{1,0:T(8,128)S(1)} fusion(bf16[512,1536]{0,1:T(8,128)(2,1)S(1)} %pad_maximum_fusion, bf16[1536,2048]{1,0:T(8,128)(2,1)S(1)} %bitcast.46), kind=kOutput, calls=%fused_computation.47 | convolution fusion | flops 3221225472 | bytes 12058624 | tf_op jit(solution)/shard_map/dot_general | solution.py:349
  301.7 1.5 fusion.3
  (63 shorter events, 11.3 us)
Async XLA Ops:
  6.5 4.1 %copy-start = (bf16[256,2048]{1,0:T(8,128)(2,1)S(1)}, bf16[256,2048]{1,0:T(8,128)(2,1)}, u32[]{:S(2)}) copy-start(bf16[256,2048]{1,0:T(8,128)(2,1)} %tokens_ref) | copy-start | bytes 3145732
  6.5 73.9 %all-gather.3.cloned.1.call-start = ((), (), s32[]{:S(2)}) async-start(), calls=%async_computation.3 | async-start | bytes 2228224 | tf_op jit(solution)/shard_map/all_gather | solution.py:304
  11.2 25.0 %collective-permute-start.4 = (bf16[256,2048]{1,0:T(8,128)(2,1)S(1)}, bf16[256,2048]{1,0:T(8,128)(2,1)S(1)}, u32[]{:S(2)}, u32[]{:S(2)}) collective-permute-start(bf16[256,2048]{1,0:T(8,128)(2,1)S(1)} %fusion.1.refs_0_), channel_id=1, source_target_pairs={{0,32},{16,48},{32,0},{48,16},{64,96},{80,112},{96,64},{112,80},{1... | collective-permute-start | bytes 3145736 | tf_op jit(solution)/shard_map/ppermute | solution.py:23
  11.6 35.5 %all-to-all-start = ((bf16[16,128,512]{2,1,0:T(8,128)(2,1)}), bf16[16,128,512]{2,1,0:T(8,128)(2,1)}, u32[]{:S(2)}, u32[]{:S(2)}) async-start(bf16[16,128,512]{2,1,0:T(8,128)(2,1)} %broadcast_in_dim.65), calls=%async_computation | async-start | bytes 4194304 | tf_op jit(solution)/shard_map/all_to_all | solution.py:311
  18.8 28.4 %collective-permute-start.3 = (bf16[256,2048]{1,0:T(8,128)(2,1)S(1)}, bf16[256,2048]{1,0:T(8,128)(2,1)}, u32[]{:S(2)}, u32[]{:S(2)}) collective-permute-start(bf16[256,2048]{1,0:T(8,128)(2,1)S(1)} %fusion.1.refs_0_), channel_id=1, source_target_pairs={{0,16},{16,0},{32,48},{48,32},{64,80},{80,64},{96,112},{112,96},{1... | collective-permute-start | bytes 3145736 | tf_op jit(solution)/shard_map/ppermute | solution.py:23
  36.1 17.0 %copy-start.2 = (bf16[256,2048]{1,0:T(8,128)(2,1)}, bf16[256,2048]{1,0:T(8,128)(2,1)S(1)}, u32[]{:S(2)}) copy-start(bf16[256,2048]{1,0:T(8,128)(2,1)S(1)} %collective-permute-done.4.refs_2_) | copy-start | bytes 3145732
  36.1 11.0 %collective-permute-start.5 = (bf16[256,2048]{1,0:T(8,128)(2,1)S(1)}, bf16[256,2048]{1,0:T(8,128)(2,1)}, u32[]{:S(2)}, u32[]{:S(2)}) collective-permute-start(bf16[256,2048]{1,0:T(8,128)(2,1)S(1)} %collective-permute-done.4.refs_2_), channel_id=1, source_target_pairs={{0,16},{16,0},{32,48},{48,32},{64,80},{80,64},{96,112},{112,96},{1... | collective-permute-start | bytes 3145736 | tf_op jit(solution)/shard_map/ppermute | solution.py:23
  37.7 5.6 %collective-permute-start.2 = (f32[2,128,128]{2,1,0:T(8,128)S(1)}, f32[2,128,128]{2,1,0:T(8,128)S(1)}, u32[]{:S(2)}, u32[]{:S(2)}) collective-permute-start(f32[2,128,128]{2,1,0:T(8,128)S(1)} %get-tuple-element.66), channel_id=1, source_target_pairs={{0,48},{16,32},{32,16},{48,0},{64,112},{80,96},{96,80},{112,64},{1... | collective-permute-start | bytes 393224 | tf_op jit(solution)/shard_map/ppermute | solution.py:23
  37.9 5.4 %collective-permute-start = (f32[2,128,128]{2,1,0:T(8,128)S(1)}, f32[2,128,128]{2,1,0:T(8,128)S(1)}, u32[]{:S(2)}, u32[]{:S(2)}) collective-permute-start(f32[2,128,128]{2,1,0:T(8,128)S(1)} %get-tuple-element.67), channel_id=1, source_target_pairs={{0,16},{16,0},{32,48},{48,32},{64,80},{80,64},{96,112},{112,96},{1... | collective-permute-start | bytes 393224 | tf_op jit(solution)/shard_map/ppermute | solution.py:23
  38.3 8.2 %collective-permute-start.1 = (f32[2,128,128]{2,1,0:T(8,128)S(1)}, f32[2,128,128]{2,1,0:T(8,128)}, u32[]{:S(2)}, u32[]{:S(2)}) collective-permute-start(f32[2,128,128]{2,1,0:T(8,128)S(1)} %get-tuple-element.69), channel_id=1, source_target_pairs={{0,32},{16,48},{32,0},{48,16},{64,96},{80,112},{96,64},{112,80},{1... | collective-permute-start | bytes 393224 | tf_op jit(solution)/shard_map/ppermute | solution.py:23
  43.2 0.7 copy-start.8
  43.9 0.6 copy-start.9
  53.2 1.0 copy-start.4
  54.2 0.8 copy-start.6
  55.0 15.6 %collective-permute-start.8 = (bf16[4,2,128,128]{3,2,1,0:T(8,128)(2,1)S(1)}, bf16[4,2,128,128]{3,2,1,0:T(8,128)(2,1)S(1)}, u32[]{:S(2)}, u32[]{:S(2)}) collective-permute-start(bf16[4,2,128,128]{3,2,1,0:T(8,128)(2,1)S(1)} %get-tuple-element.33), channel_id=1, source_target_pairs={{0,3},{1,0},{2,1},{3,2},{4,7},{5,4},{6,5},{7,6},{8,11},{9,8},{10,9... | collective-permute-start | bytes 786440 | tf_op jit(solution)/shard_map/ppermute | solution.py:32
  56.1 18.6 %collective-permute-start.7 = (bf16[4,2,128,128]{3,2,1,0:T(8,128)(2,1)S(1)}, bf16[4,2,128,128]{3,2,1,0:T(8,128)(2,1)S(1)}, u32[]{:S(2)}, u32[]{:S(2)}) collective-permute-start(bf16[4,2,128,128]{3,2,1,0:T(8,128)(2,1)S(1)} %get-tuple-element.33), channel_id=1, source_target_pairs={{0,2},{1,3},{2,0},{3,1},{4,6},{5,7},{6,4},{7,5},{8,10},{9,11},{10,... | collective-permute-start | bytes 786440 | tf_op jit(solution)/shard_map/ppermute | solution.py:32
  58.7 19.5 %collective-permute-start.6 = (bf16[4,2,128,128]{3,2,1,0:T(8,128)(2,1)S(1)}, bf16[4,2,128,128]{3,2,1,0:T(8,128)(2,1)S(1)}, u32[]{:S(2)}, u32[]{:S(2)}) collective-permute-start(bf16[4,2,128,128]{3,2,1,0:T(8,128)(2,1)S(1)} %get-tuple-element.33), channel_id=1, source_target_pairs={{0,1},{1,2},{2,3},{3,0},{4,5},{5,6},{6,7},{7,4},{8,9},{9,10},{10,1... | collective-permute-start | bytes 786440 | tf_op jit(solution)/shard_map/ppermute | solution.py:32
  80.5 6.5 %copy-start.10 = (s32[256,4]{0,1:T(4,128)S(1)}, s32[256,4]{0,1:T(4,128)}, u32[]{:S(2)}) copy-start(s32[256,4]{0,1:T(4,128)} %param.12) | copy-start | bytes 12292
  80.5 6.5 %copy-start.11 = (f32[256,4]{0,1:T(4,128)S(1)}, f32[256,4]{0,1:T(4,128)}, u32[]{:S(2)}) copy-start(f32[256,4]{0,1:T(4,128)} %param.13) | copy-start | bytes 12292
  83.2 24.4 %collective-permute-start.9 = (bf16[16,128,256]{2,1,0:T(8,128)(2,1)}, bf16[16,128,256]{2,1,0:T(8,128)(2,1)}, u32[]{:S(2)}, u32[]{:S(2)}) collective-permute-start(bf16[16,128,256]{2,1,0:T(8,128)(2,1)} %get-tuple-element.56.refs_4_), channel_id=1, source_target_pairs={{0,32},{16,48},{32,0},{48,16},{64,96},{80,112},{96,64},{112,80},{1... | collective-permute-start | bytes 3145736 | tf_op jit(solution)/shard_map/ppermute | solution.py:23
  83.6 11.5 %collective-permute-start.12 = (bf16[4,2,128,128]{3,2,1,0:T(8,128)(2,1)}, bf16[4,2,128,128]{3,2,1,0:T(8,128)(2,1)S(1)}, u32[]{:S(2)}, u32[]{:S(2)}) collective-permute-start(bf16[4,2,128,128]{3,2,1,0:T(8,128)(2,1)} %get-tuple-element.42), channel_id=1, source_target_pairs={{0,12},{1,13},{2,14},{3,15},{4,0},{5,1},{6,2},{7,3},{8,4},{9,5},{1... | collective-permute-start | bytes 786440 | tf_op jit(solution)/shard_map/ppermute | solution.py:32
  84.5 11.1 %collective-permute-start.11 = (bf16[4,2,128,128]{3,2,1,0:T(8,128)(2,1)}, bf16[4,2,128,128]{3,2,1,0:T(8,128)(2,1)}, u32[]{:S(2)}, u32[]{:S(2)}) collective-permute-start(bf16[4,2,128,128]{3,2,1,0:T(8,128)(2,1)} %get-tuple-element.42), channel_id=1, source_target_pairs={{0,8},{1,9},{2,10},{3,11},{4,12},{5,13},{6,14},{7,15},{8,0},{9,1},... | collective-permute-start | bytes 786440 | tf_op jit(solution)/shard_map/ppermute | solution.py:32
  86.9 11.9 %collective-permute-start.10 = (bf16[4,2,128,128]{3,2,1,0:T(8,128)(2,1)}, bf16[4,2,128,128]{3,2,1,0:T(8,128)(2,1)}, u32[]{:S(2)}, u32[]{:S(2)}) collective-permute-start(bf16[4,2,128,128]{3,2,1,0:T(8,128)(2,1)} %get-tuple-element.42), channel_id=1, source_target_pairs={{0,4},{1,5},{2,6},{3,7},{4,8},{5,9},{6,10},{7,11},{8,12},{9,13},{1... | collective-permute-start | bytes 786440 | tf_op jit(solution)/shard_map/ppermute | solution.py:32
  87.0 23.8 %collective-permute-start.16 = (bf16[16,128,256]{2,1,0:T(8,128)(2,1)}, bf16[16,128,256]{2,1,0:T(8,128)(2,1)S(1)}, u32[]{:S(2)}, u32[]{:S(2)}) collective-permute-start(bf16[16,128,256]{2,1,0:T(8,128)(2,1)} %get-tuple-element.56.refs_4_), channel_id=1, source_target_pairs={{0,16},{16,0},{32,48},{48,32},{64,80},{80,64},{96,112},{112,96},{1... | collective-permute-start | bytes 3145736 | tf_op jit(solution)/shard_map/ppermute | solution.py:23
  87.1 1.2 copy-start.3
  88.3 1.2 copy-start.5
  89.5 9.3 %copy-start.1 = (f32[4,2,128,128]{3,2,1,0:T(8,128)S(1)}, f32[4,2,128,128]{3,2,1,0:T(8,128)}, u32[]{:S(2)}) copy-start(f32[4,2,128,128]{3,2,1,0:T(8,128)} %get-tuple-element.57.base_ref) | copy-start | bytes 1572868
  107.6 9.2 %collective-permute-start.17 = (bf16[16,128,256]{2,1,0:T(8,128)(2,1)}, bf16[16,128,256]{2,1,0:T(8,128)(2,1)S(1)}, u32[]{:S(2)}, u32[]{:S(2)}) collective-permute-start(bf16[16,128,256]{2,1,0:T(8,128)(2,1)} %collective-permute-done.9.refs_6_), channel_id=1, source_target_pairs={{0,16},{16,0},{32,48},{48,32},{64,80},{80,64},{96,112},{112,96},{1... | collective-permute-start | bytes 3145736 | tf_op jit(solution)/shard_map/ppermute | solution.py:23
  108.2 5.2 %collective-permute-start.15 = (bf16[256,256]{1,0:T(8,128)(2,1)S(1)}, bf16[256,256]{1,0:T(8,128)(2,1)S(1)}, u32[]{:S(2)}, u32[]{:S(2)}) collective-permute-start(bf16[256,256]{1,0:T(8,128)(2,1)S(1)} %get-tuple-element.62), channel_id=1, source_target_pairs={{0,48},{16,32},{32,16},{48,0},{64,112},{80,96},{96,80},{112,64},{1... | collective-permute-start | bytes 393224 | tf_op jit(solution)/shard_map/ppermute | solution.py:23
  108.7 8.2 %collective-permute-start.14 = (bf16[256,256]{1,0:T(8,128)(2,1)S(1)}, bf16[256,256]{1,0:T(8,128)(2,1)S(1)}, u32[]{:S(2)}, u32[]{:S(2)}) collective-permute-start(bf16[256,256]{1,0:T(8,128)(2,1)S(1)} %get-tuple-element.63), channel_id=1, source_target_pairs={{0,32},{16,48},{32,0},{48,16},{64,96},{80,112},{96,64},{112,80},{1... | collective-permute-start | bytes 393224 | tf_op jit(solution)/shard_map/ppermute | solution.py:23
  110.4 6.5 %collective-permute-start.13 = (bf16[256,256]{1,0:T(8,128)(2,1)S(1)}, bf16[256,256]{1,0:T(8,128)(2,1)S(1)}, u32[]{:S(2)}, u32[]{:S(2)}) collective-permute-start(bf16[256,256]{1,0:T(8,128)(2,1)S(1)} %get-tuple-element.64), channel_id=1, source_target_pairs={{0,16},{16,0},{32,48},{48,32},{64,80},{80,64},{96,112},{112,96},{1... | collective-permute-start | bytes 393224 | tf_op jit(solution)/shard_map/ppermute | solution.py:23
  122.6 75.9 %copy-start.7 = (bf16[1,1024,2048]{2,1,0:T(8,128)(2,1)S(1)}, bf16[1,1024,2048]{2,1,0:T(8,128)(2,1)}, u32[]{:S(2)}) copy-start(bf16[1,1024,2048]{2,1,0:T(8,128)(2,1)} %param.15) | copy-start | bytes 12582916
Sparse Core Ops, SparseCore 0:
  9.5 70.7 all-gather.2

commit v3 on v2

--- a/solution.py
+++ b/solution.py
@@ -12,6 +12,7 @@
 GROUP = 4
 ROW_TILE = 512
 VMEM_LIMIT = 36 << 20
+HIGH_VMEM_LIMIT = 58 << 20
 EPSILON = 1e-05
 
 
@@ -43,9 +44,9 @@
     slot = jnp.dot(earlier, member.astype(jnp.bfloat16), preferred_element_type=jnp.float32)
     slot = jnp.where(member, slot.astype(jnp.int32), -1)
     slots = jnp.arange(capacity, dtype=jnp.int32)
-    taken_out = slot.T[:, None, :] == slots[None, :, None]
+    taken = slot.T[:, None, :] == slots[None, :, None]
+    send = taken.astype(jnp.bfloat16).reshape(experts * capacity, rows)
     taken_back = slot[:, :, None] == slots[None, None, :]
-    send = taken_out.astype(jnp.bfloat16).reshape(experts * capacity, rows)
     high = gate.astype(jnp.bfloat16)
     low = (gate - high.astype(jnp.float32)).astype(jnp.bfloat16)
     zero = jnp.zeros((), jnp.bfloat16)
@@ -61,11 +62,15 @@
     return pl.BlockSpec(a.shape, lambda i: (0,) * a.ndim)
 
 
+def slab_of(a, n):
+    return pl.BlockSpec((a.shape[0], 128, a.shape[2]), lambda i: (0, n, 0))
+
+
 def one_of(a):
     return pl.BlockSpec((1,) + a.shape[1:], lambda i: (i,) + (0,) * (a.ndim - 1))
 
 
-def call(kernel, name, grid, inputs, in_specs, outputs, out_specs, flops, scratch=()):
+def call(kernel, name, grid, inputs, in_specs, outputs, out_specs, flops, scratch=(), aliases={}, limit=VMEM_LIMIT):
     size = lambda a: a.size * a.dtype.itemsize
     return pl.pallas_call(
         kernel,
@@ -74,7 +79,8 @@
         out_specs=out_specs,
         out_shape=outputs,
         scratch_shapes=list(scratch),
-        compiler_params=pltpu.CompilerParams(vmem_limit_bytes=VMEM_LIMIT),
+        input_output_aliases=aliases,
+        compiler_params=pltpu.CompilerParams(vmem_limit_bytes=limit),
         cost_estimate=pl.CostEstimate(
             flops=flops,
             bytes_accessed=sum(size(a) for a in inputs) + sum(size(a) for a in outputs),
@@ -86,6 +92,47 @@
 
 def out_like(shape, dtype):
     return jax.ShapeDtypeStruct(shape, dtype)
+
+
+def prepare_kernel(where_ref, tokens_ref, qkv_ref, out_ref, spread_ref, second_ref, normed_ref):
+    own_width = second_ref.shape[1]
+    width_heads = HEADS * HD
+    shard_rows = qkv_ref.shape[0]
+    share = out_ref.shape[1] // 2
+    at = lambda start, size: pl.ds(pl.multiple_of(start, size), size)
+    part = lambda n: qkv_ref[:, at(n * width_heads + where_ref[0] * own_width, own_width)]
+    normed_ref[...] = rms_rows(tokens_ref[...].astype(jnp.float32)).astype(jnp.bfloat16)
+    keys, values = part(1), part(2)
+    for n in range(spread_ref.shape[0]):
+        spread_ref[n, :, :own_width] = keys
+        spread_ref[n, :, own_width:] = values
+
+    @pl.when(pl.program_id(0) == 0)
+    def _():
+        second_ref[:shard_rows] = part(0)
+        rows = out_ref.shape[0]
+        for n in range(share // own_width):
+            columns = at((where_ref[0] & 1) * share + n * own_width, own_width)
+            second_ref[shard_rows + n * rows : shard_rows + (n + 1) * rows] = out_ref[:, columns]
+
+
+def prepared(place, tokens, qkv_weight, out_weight, own_width, experts):
+    steps = 4
+    rows, width = tokens.shape
+    stacked = qkv_weight.shape[0] + out_weight.shape[0] * (width // 2 // own_width)
+    inputs = [place.reshape(1), tokens, qkv_weight, out_weight]
+    outputs = [
+        out_like((experts, qkv_weight.shape[0], 2 * own_width), jnp.bfloat16),
+        out_like((stacked, own_width), jnp.bfloat16),
+        out_like((rows, width), jnp.bfloat16),
+    ]
+    slab = lambda a: pl.BlockSpec((a.shape[0] // steps,) + a.shape[1:], lambda i: (i,) + (0,) * (a.ndim - 1))
+    return call(
+        prepare_kernel, "prepared", steps, inputs,
+        [pl.BlockSpec(memory_space=pltpu.SMEM), slab(tokens), whole(qkv_weight), whole(out_weight)],
+        outputs, [slab(outputs[0]), whole(outputs[1]), slab(outputs[2])], 4 * tokens.size,
+        limit=HIGH_VMEM_LIMIT,
+    )
 
 
 def key_value_kernel(w_ref, *refs):
@@ -130,13 +177,14 @@
 
 def query_kernel(w_ref, pair_ref, *refs):
     rows_refs, (query_ref, inside_ref) = refs[:GROUP], refs[GROUP:]
-    own_width = w_ref.shape[1]
+    own_width = w_ref.shape[2]
     rows = pair_ref.shape[1]
     for j, x_ref in enumerate(rows_refs):
 
         @pl.when(pl.program_id(0) == j)
         def _(x_ref=x_ref):
-            query_ref[0] = jax.nn.silu(dot32(x_ref[...], w_ref[...])).astype(jnp.bfloat16)
+            weight = w_ref[...].reshape(-1, own_width)
+            query_ref[0] = jax.nn.silu(dot32(x_ref[...], weight)).astype(jnp.bfloat16)
 
     causal = lax.broadcasted_iota(jnp.int32, (rows, rows), 0) >= lax.broadcasted_iota(
         jnp.int32, (rows, rows), 1
@@ -156,7 +204,7 @@
 
 def queries_inside(weight, pair, everyone):
     rows, width = everyone[0].shape
-    own_width = weight.shape[1]
+    own_width = weight.shape[2]
     inputs = [weight, pair, *everyone]
     outputs = [
         out_like((GROUP, rows, own_width), jnp.bfloat16),
@@ -165,7 +213,7 @@
     flops = 2 * GROUP * rows * own_width * (width + 2 * rows)
     return call(
         query_kernel, "queries_inside", GROUP, inputs,
-        [whole(weight), one_of(pair)] + [whole(a) for a in everyone],
+        [slab_of(weight, 0), one_of(pair)] + [whole(a) for a in everyone],
         outputs, [one_of(a) for a in outputs], flops,
     )
 
@@ -196,22 +244,25 @@
 
 
 def project_kernel(where_ref, tokens_ref, send_ref, *refs):
-    back, quarters = refs[:GROUP], refs[GROUP : 2 * GROUP]
-    hidden_ref, rows_ref, ordered_ref, sum_ref, normed_ref = refs[2 * GROUP :]
+    back, slabs = refs[:GROUP], refs[GROUP : GROUP + 4]
+    hidden_ref, rows_ref, ordered_ref, sum_ref, normed_ref = refs[GROUP + 4 :]
     own_width = back[0].shape[1]
-    count, twice, narrow = quarters[0].shape
-    half = twice // 2
-
-    @pl.when(pl.program_id(0) == 0)
+    count, stacked, narrow = slabs[0].shape
+    shard = ordered_ref.shape[1] // count
+    parts = stacked // shard
+    step = pl.program_id(0)
+
+    @pl.when(step == 0)
     def _():
         for j, ref in enumerate(back):
             at = pl.multiple_of((where_ref[0] ^ j) * own_width, own_width)
             ordered_ref[:, pl.ds(at, own_width)] = ref[...]
         heads = ordered_ref[...]
-        for j, ref in enumerate(quarters):
-            for n in range(2):
-                weight = ref[:, n * half : (n + 1) * half, :].reshape(count * half, narrow)
-                at = pl.multiple_of(((where_ref[0] ^ j) * 2 + n) * narrow, narrow)
+        for j, ref in enumerate(slabs):
+            for n in range(parts):
+                weight = ref[:, n * shard : (n + 1) * shard, :].reshape(count * shard, narrow)
+                at = ((where_ref[0] & 1) ^ (j // 2)) * 2 * parts + j % 2 * parts + n
+                at = pl.multiple_of(at * narrow, narrow)
                 sum_ref[:, pl.ds(at, narrow)] = dot32(heads, weight)
         hidden = (tokens_ref[...].astype(jnp.float32) + sum_ref[...]).astype(jnp.bfloat16)
         hidden_ref[...] = hidden
@@ -220,23 +271,31 @@
     rows_ref[...] = dot32(send_ref[...], normed_ref[...]).astype(jnp.bfloat16)
 
 
-def projected_rows(place, tokens, send, back, quarters):
+def projected_rows(place, tokens, send, back, halves):
     rows, width = tokens.shape
     slots = send.shape[0]
-    tile = slots // 4
-    inputs = [place.reshape(1), tokens, send, *back, *quarters]
+    tile = 384
+    inputs = [place.reshape(1), tokens, send, *back, halves[0], halves[0], halves[1], halves[1]]
     specs = [pl.BlockSpec(memory_space=pltpu.SMEM), whole(tokens)]
     specs += [pl.BlockSpec((tile, rows), lambda i: (i, 0))]
-    specs += [whole(a) for a in inputs[3:]]
-    outputs = [out_like((rows, width), jnp.bfloat16), out_like((slots, width), jnp.bfloat16)]
-    out_specs = [whole(outputs[0]), pl.BlockSpec((tile, width), lambda i: (i, 0))]
+    specs += [whole(a) for a in back] + [slab_of(a, n) for a in halves for n in (1, 2)]
+    outputs = [
+        out_like((rows, width), jnp.bfloat16),
+        out_like((slots, width), jnp.bfloat16),
+    ]
+    out_specs = [
+        whole(outputs[0]),
+        pl.BlockSpec((tile, width), lambda i: (i, 0)),
+    ]
     scratch = [
         pltpu.VMEM((rows, GROUP * back[0].shape[1]), jnp.bfloat16),
         pltpu.VMEM((rows, width), jnp.float32),
         pltpu.VMEM((rows, width), jnp.bfloat16),
     ]
     flops = 2 * rows * width * (slots + GROUP * back[0].shape[1])
-    return call(project_kernel, "projected_rows", 4, inputs, specs, outputs, out_specs, flops, scratch)
+    return call(
+        project_kernel, "projected_rows", slots // tile, inputs, specs, outputs, out_specs, flops, scratch
+    )
 
 
 def expert_kernel(rows_ref, gate_ref, up_ref, out_weight_ref, out_ref, middle_ref):
@@ -294,18 +353,9 @@
     column = lax.axis_index("ctx") // SIDE
     row = lax.axis_index("ctx") % SIDE
     cut = lambda a, start, size, axis: lax.dynamic_slice_in_dim(a, start, size, axis=axis)
-    shard_rows = qkv_weight.shape[0]
-
-    part = lambda n: cut(qkv_weight, n * width_heads + place * own_width, own_width, 1)
-    first = jnp.concatenate([part(1), part(2)], axis=1)
-    out_part = cut(out_weight, place * (width // GROUP), width // GROUP, 1)
-    out_parts = jnp.split(out_part, width // GROUP // own_width, axis=1)
-    second = jnp.concatenate([part(0)] + out_parts, axis=0)
+
+    spread, second, normed = prepared(place, tokens, qkv_weight, out_weight, own_width, experts)
     second = lax.all_gather(second[None], "ctx", axis=0, tiled=True)
-
-    spread = jnp.broadcast_to(first[None], (experts,) + first.shape)
-    spread, tokens = lax.optimization_barrier((spread, tokens))
-    normed = rms_rows(tokens.astype(jnp.float32)).astype(jnp.bfloat16)
     far = swap_with(normed, 2)
     near = swap_with(normed, 1)
     first = lax.all_to_all(spread, "ctx", split_axis=0, concat_axis=0, tiled=True)
@@ -313,7 +363,8 @@
     prior = [cut(prior_state, place * own_heads, own_heads, 0)]
     for other in range(1, GROUP):
         prior.append(swap_with(cut(prior_state, (place ^ other) * own_heads, own_heads, 0), other))
-    first, prior = lax.optimization_barrier((first, tuple(prior)))
+    send, weigh = routing(expert_ids, gate_weights, experts, capacity)
+    first, prior, send, weigh = lax.optimization_barrier((first, tuple(prior), send, weigh))
     prior = jnp.stack(prior)
 
     pair, state, sent = keys_values_states(first.reshape(width, 2 * own_width), everyone)
@@ -323,19 +374,14 @@
     for d in range(1, SIDE):
         base = base + jnp.where(row >= d, in_row[d - 1], 0.0)
 
-    second, total = lax.optimization_barrier((second, total))
+    second, _ = lax.optimization_barrier((second, total))
     across = [shift_ctx(total, d, 0) for d in range(1, SIDE)]
-    query, inside = queries_inside(second[:, :shard_rows].reshape(width, own_width), pair, everyone)
-    quarter = second[:, shard_rows:]
-    quarter_far = swap_with(quarter, 2)
-    quarter_near = swap_with(quarter, 1)
-    send, weigh = routing(expert_ids, gate_weights, experts, capacity)
+    query, inside = queries_inside(second, pair, everyone)
+    halves = [second, swap_with(second, 1)]
 
     head_normed = finished_heads(column, query, inside, base, across)
-    quarter_far, head_normed = lax.optimization_barrier((quarter_far, head_normed))
-    quarters = [quarter, quarter_near, quarter_far, swap_with(quarter_far, 1)]
     back = [head_normed[0]] + [swap_with(head_normed[j], j) for j in range(1, GROUP)]
-    hidden, outgoing = projected_rows(place, tokens, send, back, quarters)
+    hidden, outgoing = projected_rows(place, tokens, send, back, halves)
 
     outgoing, weigh, hidden = lax.optimization_barrier((outgoing, weigh, hidden))
     outgoing = outgoing.reshape(experts, capacity, width)

time: 315 us -> 310 us (0.984)
  waiting for transfers between devices: 57.4 us -> 51 us
  local copies, waits for them, and re-layouts: 13.2 us -> 8.04 us
  Pallas kernels: 43.7 us -> 47.2 us
    ppermute x12 -> x10, waiting for transfers between devices: 34.6 us -> 26.5 us  [swap_with(): lax.ppermute(x, 'dp', [(i, i ^ mask) for i in range(lax.axis_size('dp'))])]
    pallas_call x5 -> x6, Pallas kernels: 43.7 us -> 47.2 us  [call(): pl.pallas_call(kernel, grid=(grid,), in_specs=in_specs, out_specs=out_spe...]
  transfers between devices with their start and end apart: 20 -> 18, of which waited for: 12 -> 10; matrix products, arithmetic and copies ran while one was open for 2% -> 3% of each run, Pallas kernels for 5% -> 5%
where the time goes in v3:
time: 310 us; the launch traced here: 305 us
  blocking collectives  153 us (49%)
  waiting for transfers between devices  51 us (16%)
  Pallas kernels  47.2 us (15%)
  starting transfers between devices  20.2 us (7%)
  between operations  13.6 us (4%)
  other arithmetic  8.11 us (3%)
  local copies, waits for them, and re-layouts  8.04 us (3%)
  matrix products  3.65 us (1%)
    all_to_all x1, blocking collectives, shards(): lax.all_to_all(outgoing, 'ctx', split_axis=0, concat_axis=0, tiled=True)  77.4 us
    all_to_all x1, blocking collectives, shards(): lax.all_to_all(result.reshape(experts, capacity, width), 'ctx', split_axi...  75.7 us
    pallas_call x6, Pallas kernels, call(): pl.pallas_call(kernel, grid=(grid,), in_specs=in_specs, out_specs=out_spe...  47.2 us
    ppermute x10, waiting for transfers between devices, swap_with(): lax.ppermute(x, 'dp', [(i, i ^ mask) for i in range(lax.axis_size('dp'))])  26.5 us
    ppermute x6, waiting for transfers between devices, shift_ctx(): return lax.ppermute(x, 'ctx', pairs)  23.3 us
    ppermute x6, starting transfers between devices, shift_ctx(): return lax.ppermute(x, 'ctx', pairs)  8.31 us
    all_to_all x1, starting transfers between devices, shards(): lax.all_to_all(spread, 'ctx', split_axis=0, concat_axis=0, tiled=True)  7.24 us
  transfers between devices with their start and end apart: 18, of which 10 were waited for; matrix products, arithmetic and copies ran while one was open for 3% of the time, Pallas kernels for 5%

profile of v3, /device:TPU:124, one launch (start us, length us, event | category | flops | bytes accessed | tf_op | source)
XLA Modules:
  0.0 304.9 jit_solution(17123140699416153223)
XLA Ops:
  6.5 4.4 %prepared.1 = (bf16[16,128,512]{2,1,0:T(8,128)(2,1)}, bf16[384,256]{1,0:T(8,128)(2,1)}, bf16[256,2048]{1,0:T(8,128)(2,1)}) custom-call(s32[1]{0:T(128)} %bitcast.where_ref, bf16[256,2048]{1,0:T(8,128)(2,1)} %tokens_ref.3, bf16[128,3072]{1,0:T(8,128)(2,1)} %qkv_ref.1, bf16[64,2048]{1,0:T(8,128)(2,1)} %out_ref.1), custom_call_target="tpu_custom_call" | custom-call | flops 2097152 | bytes 5439492 | tf_op jit(solution)/shard_map/prepared/pallas_call | solution.py:75
  11.5 7.2 %all-to-all-start = ((bf16[16,128,512]{2,1,0:T(8,128)(2,1)}), bf16[16,128,512]{2,1,0:T(8,128)(2,1)S(1)}, u32[]{:S(2)}, u32[]{:S(2)}) async-start(bf16[16,128,512]{2,1,0:T(8,128)(2,1)} %get-tuple-element.29), calls=%async_computation | async-start | bytes 4194304 | tf_op jit(solution)/shard_map/all_to_all | solution.py:361
  18.8 17.4 %collective-permute-done.4.refs_2_ = bf16[256,2048]{1,0:T(8,128)(2,1)} collective-permute-done((bf16[256,2048]{1,0:T(8,128)(2,1)}, bf16[256,2048]{1,0:T(8,128)(2,1)}, u32[]{:S(2)}, u32[]{:S(2)}) %collective-permute-start.4) | collective-permute-done | bytes 1048608 | tf_op jit(solution)/shard_map/ppermute | solution.py:24
  36.3 1.8 constant_dynamic-slice_fusion
  38.6 1.6 collective-permute-start.1
  42.2 1.3 pad_maximum_fusion
  43.5 1.2 fusion.4.send_ref
  44.7 2.3 collective-permute-done.1
  47.0 1.1 all-to-all-done
  48.1 5.7 %keys_values_states.1 = (bf16[4,256,512]{2,1,0:T(8,128)(2,1)S(1)}, f32[4,2,128,128]{3,2,1,0:T(8,128)S(1)}, bf16[4,2,128,128]{3,2,1,0:T(8,128)(2,1)S(1)}) custom-call(bf16[2048,512]{1,0:T(8,128)(2,1)S(1)} %bitcast.47, bf16[256,2048]{1,0:T(8,128)(2,1)S(1)} %copy-done.5, bf16[256,2048]{1,0:T(8,128)(2,1)} %collective-permute-done.3.refs_1_, ...), custom_call_target="tpu_custom_call" | custom-call | flops 2147483648 | bytes 8126464 | tf_op jit(solution)/shard_map/keys_values_states/pallas_call | solution.py:75
  55.6 1.2 collective-permute-start.8
  56.7 2.5 collective-permute-start.7
  59.2 1.2 collective-permute-start.6
  60.4 12.1 %collective-permute-done.8 = bf16[4,2,128,128]{3,2,1,0:T(8,128)(2,1)S(1)} collective-permute-done((bf16[4,2,128,128]{3,2,1,0:T(8,128)(2,1)S(1)}, bf16[4,2,128,128]{3,2,1,0:T(8,128)(2,1)S(1)}, u32[]{:S(2)}, u32[]{:S(2)}) %collective-permute-start.8) | collective-permute-done | bytes 262176 | tf_op jit(solution)/shard_map/ppermute | solution.py:33
  72.6 5.7 %collective-permute-done.7 = bf16[4,2,128,128]{3,2,1,0:T(8,128)(2,1)S(1)} collective-permute-done((bf16[4,2,128,128]{3,2,1,0:T(8,128)(2,1)S(1)}, bf16[4,2,128,128]{3,2,1,0:T(8,128)(2,1)S(1)}, u32[]{:S(2)}, u32[]{:S(2)}) %collective-permute-start.7) | collective-permute-done | bytes 262176 | tf_op jit(solution)/shard_map/ppermute | solution.py:33
  78.3 2.8 collective-permute-done.6
  81.1 2.4 fusion.8
  84.2 2.7 collective-permute-start.10
  87.1 1.9 copy-done
  88.9 1.2 copy-done.6
  90.2 1.2 copy-done.8
  91.4 6.0 %queries_inside.1 = (bf16[4,256,256]{2,1,0:T(8,128)(2,1)S(1)}, f32[4,256,256]{2,1,0:T(8,128)S(1)}) custom-call(bf16[16,384,256]{2,1,0:T(8,128)(2,1)S(1)} %bitcast.41, bf16[4,256,512]{2,1,0:T(8,128)(2,1)S(1)} %copy-done.8, bf16[256,2048]{1,0:T(8,128)(2,1)S(1)} %copy-done.6, bf16[256,2048]{1,0:T(8,128)(2,1)} %collective-permute-done.3.refs_1_, ...), custom_call_target="tpu_custom_call" | custom-call | flops 1342177280 | bytes 9961472 | tf_op jit(solution)/shard_map/queries_inside/pallas_call | solution.py:75
  97.4 2.6 collective-permute-done.9.refs_0_
  100.1 3.1 %finished_heads.1 = bf16[4,256,256]{2,1,0:T(8,128)(2,1)S(1)} custom-call(s32[1]{0:T(128)} %bitcast.6.where_ref, bf16[4,256,256]{2,1,0:T(8,128)(2,1)S(1)} %get-tuple-element.38.query_ref, f32[4,256,256]{2,1,0:T(8,128)S(1)} %get-tuple-element.39.inside_ref, f32[4,2,128,128]{3,2,1,0:T(8,128)S(1)} %copy-done.4, ...), custom_call_target="tpu_custom_call" | custom-call | flops 134217728 | bytes 3407876 | tf_op jit(solution)/shard_map/finished_heads/pallas_call | solution.py:75
  105.2 3.7 %collective-permute-done.14.refs_3_ = bf16[256,256]{1,0:T(8,128)(2,1)S(1)} collective-permute-done((bf16[256,256]{1,0:T(8,128)(2,1)S(1)}, bf16[256,256]{1,0:T(8,128)(2,1)S(1)}, u32[]{:S(2)}, u32[]{:S(2)}) %collective-permute-start.14) | collective-permute-done | bytes 131104 | tf_op jit(solution)/shard_map/ppermute | solution.py:24
  108.9 3.0 collective-permute-done.13.refs_2_
  111.9 4.5 %projected_rows.1 = (bf16[256,2048]{1,0:T(8,128)(2,1)S(1)}, bf16[1536,2048]{1,0:T(8,128)(2,1)S(1)}) custom-call(s32[1]{0:T(128)} %bitcast.where_ref, bf16[256,2048]{1,0:T(8,128)(2,1)S(1)} %copy-done.2, bf16[1536,256]{1,0:T(8,128)(2,1)S(1)} %copy-done.3, bf16[256,256]{1,0:T(8,128)(2,1)S(1)} %get-tuple-element.60.refs_0_, ...), custom_call_target="tpu_custom_call" | custom-call | flops 2684354560 | bytes 22282244 | tf_op jit(solution)/shard_map/projected_rows/pallas_call | solution.py:75
  116.4 77.4 %all_to_all.15 = bf16[16,96,2048]{2,1,0:T(8,128)(2,1)S(1)} all-to-all(bf16[16,96,2048]{2,1,0:T(8,128)(2,1)S(1)} %bitcast.44), channel_id=1, replica_groups=mesh['dp'=8,'ctx'=16] {'ctx'}, dimensions={0} | all-to-all | bytes 12582912 | tf_op jit(solution)/shard_map/all_to_all | solution.py:388
  193.8 23.5 %expert_rows.1 = bf16[1536,2048]{1,0:T(8,128)(2,1)S(1)} custom-call(bf16[1536,2048]{1,0:T(8,128)(2,1)S(1)} %bitcast.45, bf16[2048,2048]{1,0:T(8,128)(2,1)} %bitcast.52, bf16[2048,2048]{1,0:T(8,128)(2,1)} %bitcast.53, bf16[1024,2048]{1,0:T(8,128)(2,1)S(1)} %bitcast.48), custom_call_target="tpu_custom_call" | custom-call | flops 19327352832 | bytes 33554432 | tf_op jit(solution)/shard_map/expert_rows/pallas_call | solution.py:75
  217.3 75.7 %all_to_all.16 = bf16[16,96,2048]{2,1,0:T(8,128)(2,1)S(1)} all-to-all(bf16[16,96,2048]{2,1,0:T(8,128)(2,1)S(1)} %bitcast.46), channel_id=1, replica_groups=mesh['dp'=8,'ctx'=16] {'ctx'}, dimensions={0} | all-to-all | bytes 12582912 | tf_op jit(solution)/shard_map/all_to_all | solution.py:392
  293.0 3.5 %fusion.11 = f32[512,2048]{1,0:T(8,128)S(1)} fusion(bf16[512,1536]{0,1:T(8,128)(2,1)S(1)} %copy-done.11, bf16[1536,2048]{1,0:T(8,128)(2,1)S(1)} %bitcast.49), kind=kOutput, calls=%fused_computation.34 | convolution fusion | flops 3221225472 | bytes 12058624 | tf_op jit(solution)/shard_map/dot_general | solution.py:395
  296.5 1.5 fusion.1
  (51 shorter events, 7.8 us)
Async XLA Ops:
  6.5 77.1 %all-gather.3.cloned.1.call-start = ((), (), s32[]{:S(2)}) async-start(), calls=%async_computation.3 | async-start | bytes 3342336 | tf_op jit(solution)/shard_map/all_gather | solution.py:358
  11.0 25.3 %collective-permute-start.4 = (bf16[256,2048]{1,0:T(8,128)(2,1)}, bf16[256,2048]{1,0:T(8,128)(2,1)}, u32[]{:S(2)}, u32[]{:S(2)}) collective-permute-start(bf16[256,2048]{1,0:T(8,128)(2,1)} %get-tuple-element.33.refs_0_), channel_id=1, source_target_pairs={{0,32},{16,48},{32,0},{48,16},{64,96},{80,112},{96,64},{112,80},{1... | collective-permute-start | bytes 3145736 | tf_op jit(solution)/shard_map/ppermute | solution.py:24
  11.5 7.2 %copy-start.5 = (bf16[256,2048]{1,0:T(8,128)(2,1)S(1)}, bf16[256,2048]{1,0:T(8,128)(2,1)}, u32[]{:S(2)}) copy-start(bf16[256,2048]{1,0:T(8,128)(2,1)} %get-tuple-element.33.refs_0_) | copy-start | bytes 3145732
  11.5 36.6 %all-to-all-start = ((bf16[16,128,512]{2,1,0:T(8,128)(2,1)}), bf16[16,128,512]{2,1,0:T(8,128)(2,1)S(1)}, u32[]{:S(2)}, u32[]{:S(2)}) async-start(bf16[16,128,512]{2,1,0:T(8,128)(2,1)} %get-tuple-element.29), calls=%async_computation | async-start | bytes 4194304 | tf_op jit(solution)/shard_map/all_to_all | solution.py:361
  18.7 29.3 %collective-permute-start.3 = (bf16[256,2048]{1,0:T(8,128)(2,1)S(1)}, bf16[256,2048]{1,0:T(8,128)(2,1)}, u32[]{:S(2)}, u32[]{:S(2)}) collective-permute-start(bf16[256,2048]{1,0:T(8,128)(2,1)S(1)} %copy-done.5), channel_id=1, source_target_pairs={{0,16},{16,0},{32,48},{48,32},{64,80},{80,64},{96,112},{112,96},{1... | collective-permute-start | bytes 3145736 | tf_op jit(solution)/shard_map/ppermute | solution.py:24
  36.3 11.8 %collective-permute-start.5 = (bf16[256,2048]{1,0:T(8,128)(2,1)}, bf16[256,2048]{1,0:T(8,128)(2,1)}, u32[]{:S(2)}, u32[]{:S(2)}) collective-permute-start(bf16[256,2048]{1,0:T(8,128)(2,1)} %collective-permute-done.4.refs_2_), channel_id=1, source_target_pairs={{0,16},{16,0},{32,48},{48,32},{64,80},{80,64},{96,112},{112,96},{1... | collective-permute-start | bytes 3145736 | tf_op jit(solution)/shard_map/ppermute | solution.py:24
  38.1 6.6 %collective-permute-start.2 = (f32[2,128,128]{2,1,0:T(8,128)}, f32[2,128,128]{2,1,0:T(8,128)}, u32[]{:S(2)}, u32[]{:S(2)}) collective-permute-start(f32[2,128,128]{2,1,0:T(8,128)} %get-tuple-element.61), channel_id=1, source_target_pairs={{0,48},{16,32},{32,16},{48,0},{64,112},{80,96},{96,80},{112,64},{1... | collective-permute-start | bytes 393224 | tf_op jit(solution)/shard_map/ppermute | solution.py:24
  38.6 6.1 %collective-permute-start = (f32[2,128,128]{2,1,0:T(8,128)S(1)}, f32[2,128,128]{2,1,0:T(8,128)}, u32[]{:S(2)}, u32[]{:S(2)}) collective-permute-start(f32[2,128,128]{2,1,0:T(8,128)S(1)} %get-tuple-element.62), channel_id=1, source_target_pairs={{0,16},{16,0},{32,48},{48,32},{64,80},{80,64},{96,112},{112,96},{1... | collective-permute-start | bytes 393224 | tf_op jit(solution)/shard_map/ppermute | solution.py:24
  38.6 8.4 %collective-permute-start.1 = (f32[2,128,128]{2,1,0:T(8,128)S(1)}, f32[2,128,128]{2,1,0:T(8,128)}, u32[]{:S(2)}, u32[]{:S(2)}) collective-permute-start(f32[2,128,128]{2,1,0:T(8,128)S(1)} %get-tuple-element.64), channel_id=1, source_target_pairs={{0,32},{16,48},{32,0},{48,16},{64,96},{80,112},{96,64},{112,80},{1... | collective-permute-start | bytes 393224 | tf_op jit(solution)/shard_map/ppermute | solution.py:24
  53.8 1.0 copy-start.7
  54.7 0.8 copy-start.9
  55.6 17.0 %collective-permute-start.8 = (bf16[4,2,128,128]{3,2,1,0:T(8,128)(2,1)S(1)}, bf16[4,2,128,128]{3,2,1,0:T(8,128)(2,1)S(1)}, u32[]{:S(2)}, u32[]{:S(2)}) collective-permute-start(bf16[4,2,128,128]{3,2,1,0:T(8,128)(2,1)S(1)} %get-tuple-element.35), channel_id=1, source_target_pairs={{0,3},{1,0},{2,1},{3,2},{4,7},{5,4},{6,5},{7,6},{8,11},{9,8},{10,9... | collective-permute-start | bytes 786440 | tf_op jit(solution)/shard_map/ppermute | solution.py:33
  56.7 21.5 %collective-permute-start.7 = (bf16[4,2,128,128]{3,2,1,0:T(8,128)(2,1)S(1)}, bf16[4,2,128,128]{3,2,1,0:T(8,128)(2,1)S(1)}, u32[]{:S(2)}, u32[]{:S(2)}) collective-permute-start(bf16[4,2,128,128]{3,2,1,0:T(8,128)(2,1)S(1)} %get-tuple-element.35), channel_id=1, source_target_pairs={{0,2},{1,3},{2,0},{3,1},{4,6},{5,7},{6,4},{7,5},{8,10},{9,11},{10,... | collective-permute-start | bytes 786440 | tf_op jit(solution)/shard_map/ppermute | solution.py:33
  59.2 21.8 %collective-permute-start.6 = (bf16[4,2,128,128]{3,2,1,0:T(8,128)(2,1)S(1)}, bf16[4,2,128,128]{3,2,1,0:T(8,128)(2,1)S(1)}, u32[]{:S(2)}, u32[]{:S(2)}) collective-permute-start(bf16[4,2,128,128]{3,2,1,0:T(8,128)(2,1)S(1)} %get-tuple-element.35), channel_id=1, source_target_pairs={{0,1},{1,2},{2,3},{3,0},{4,5},{5,6},{6,7},{7,4},{8,9},{9,10},{10,1... | collective-permute-start | bytes 786440 | tf_op jit(solution)/shard_map/ppermute | solution.py:33
  83.6 28.3 %collective-permute-start.15 = (bf16[16,384,256]{2,1,0:T(8,128)(2,1)}, bf16[16,384,256]{2,1,0:T(8,128)(2,1)S(1)}, u32[]{:S(2)}, u32[]{:S(2)}) collective-permute-start(bf16[16,384,256]{2,1,0:T(8,128)(2,1)} %bitcast.40), channel_id=1, source_target_pairs={{0,16},{16,0},{32,48},{48,32},{64,80},{80,64},{96,112},{112,96},{1... | collective-permute-start | bytes 9437192 | tf_op jit(solution)/shard_map/ppermute | solution.py:24
  83.6 13.8 %collective-permute-start.11 = (bf16[4,2,128,128]{3,2,1,0:T(8,128)(2,1)}, bf16[4,2,128,128]{3,2,1,0:T(8,128)(2,1)S(1)}, u32[]{:S(2)}, u32[]{:S(2)}) collective-permute-start(bf16[4,2,128,128]{3,2,1,0:T(8,128)(2,1)} %get-tuple-element.56), channel_id=1, source_target_pairs={{0,12},{1,13},{2,14},{3,15},{4,0},{5,1},{6,2},{7,3},{8,4},{9,5},{1... | collective-permute-start | bytes 786440 | tf_op jit(solution)/shard_map/ppermute | solution.py:33
  84.2 13.2 %collective-permute-start.10 = (bf16[4,2,128,128]{3,2,1,0:T(8,128)(2,1)}, bf16[4,2,128,128]{3,2,1,0:T(8,128)(2,1)}, u32[]{:S(2)}, u32[]{:S(2)}) collective-permute-start(bf16[4,2,128,128]{3,2,1,0:T(8,128)(2,1)} %get-tuple-element.56), channel_id=1, source_target_pairs={{0,8},{1,9},{2,10},{3,11},{4,12},{5,13},{6,14},{7,15},{8,0},{9,1},... | collective-permute-start | bytes 786440 | tf_op jit(solution)/shard_map/ppermute | solution.py:33
  86.9 13.2 %collective-permute-start.9 = (bf16[4,2,128,128]{3,2,1,0:T(8,128)(2,1)}, bf16[4,2,128,128]{3,2,1,0:T(8,128)(2,1)}, u32[]{:S(2)}, u32[]{:S(2)}) collective-permute-start(bf16[4,2,128,128]{3,2,1,0:T(8,128)(2,1)} %get-tuple-element.56), channel_id=1, source_target_pairs={{0,4},{1,5},{2,6},{3,7},{4,8},{5,9},{6,10},{7,11},{8,12},{9,13},{1... | collective-permute-start | bytes 786440 | tf_op jit(solution)/shard_map/ppermute | solution.py:33
  87.1 1.9 copy-start
  88.9 1.2 copy-start.6
  90.2 1.2 copy-start.8
  91.4 8.7 %copy-start.4 = (f32[4,2,128,128]{3,2,1,0:T(8,128)S(1)}, f32[4,2,128,128]{3,2,1,0:T(8,128)}, u32[]{:S(2)}) copy-start(f32[4,2,128,128]{3,2,1,0:T(8,128)} %get-tuple-element.55.base_ref) | copy-start | bytes 1572868
  91.4 20.5 %copy-start.3 = (bf16[1536,256]{1,0:T(8,128)(2,1)S(1)}, bf16[1536,256]{1,0:T(8,128)(2,1)}, u32[]{:S(2)}) copy-start(bf16[1536,256]{1,0:T(8,128)(2,1)} %fusion.4.send_ref) | copy-start | bytes 2359300
  100.1 11.8 %copy-start.1 = (bf16[6144,256]{1,0:T(8,128)(2,1)S(1)}, bf16[6144,256]{1,0:T(8,128)(2,1)}, u32[]{:S(2)}) copy-start(bf16[6144,256]{1,0:T(8,128)(2,1)} %all-gather.3.cloned.1.call-done) | copy-start | bytes 9437188
  100.1 11.9 %copy-start.2 = (bf16[256,2048]{1,0:T(8,128)(2,1)S(1)}, bf16[256,2048]{1,0:T(8,128)(2,1)}, u32[]{:S(2)}) copy-start(bf16[256,2048]{1,0:T(8,128)(2,1)} %tokens_ref.3) | copy-start | bytes 3145732
  103.2 5.7 %collective-permute-start.14 = (bf16[256,256]{1,0:T(8,128)(2,1)S(1)}, bf16[256,256]{1,0:T(8,128)(2,1)S(1)}, u32[]{:S(2)}, u32[]{:S(2)}) collective-permute-start(bf16[256,256]{1,0:T(8,128)(2,1)S(1)} %get-tuple-element.57), channel_id=1, source_target_pairs={{0,48},{16,32},{32,16},{48,0},{64,112},{80,96},{96,80},{112,64},{1... | collective-permute-start | bytes 393224 | tf_op jit(solution)/shard_map/ppermute | solution.py:24
  103.9 8.0 %collective-permute-start.13 = (bf16[256,256]{1,0:T(8,128)(2,1)S(1)}, bf16[256,256]{1,0:T(8,128)(2,1)S(1)}, u32[]{:S(2)}, u32[]{:S(2)}) collective-permute-start(bf16[256,256]{1,0:T(8,128)(2,1)S(1)} %get-tuple-element.58), channel_id=1, source_target_pairs={{0,32},{16,48},{32,0},{48,16},{64,96},{80,112},{96,64},{112,80},{1... | collective-permute-start | bytes 393224 | tf_op jit(solution)/shard_map/ppermute | solution.py:24
  104.9 7.0 %collective-permute-start.12 = (bf16[256,256]{1,0:T(8,128)(2,1)S(1)}, bf16[256,256]{1,0:T(8,128)(2,1)S(1)}, u32[]{:S(2)}, u32[]{:S(2)}) collective-permute-start(bf16[256,256]{1,0:T(8,128)(2,1)S(1)} %get-tuple-element.59), channel_id=1, source_target_pairs={{0,16},{16,0},{32,48},{48,32},{64,80},{80,64},{96,112},{112,96},{1... | collective-permute-start | bytes 393224 | tf_op jit(solution)/shard_map/ppermute | solution.py:24
  116.4 77.4 %copy-start.10 = (bf16[1,1024,2048]{2,1,0:T(8,128)(2,1)S(1)}, bf16[1,1024,2048]{2,1,0:T(8,128)(2,1)}, u32[]{:S(2)}) copy-start(bf16[1,1024,2048]{2,1,0:T(8,128)(2,1)} %param.15) | copy-start | bytes 12582916
  217.3 75.7 %copy-start.11 = (bf16[512,1536]{0,1:T(8,128)(2,1)S(1)}, bf16[512,1536]{0,1:T(8,128)(2,1)}, u32[]{:S(2)}) copy-start(bf16[512,1536]{0,1:T(8,128)(2,1)} %pad_maximum_fusion) | copy-start | bytes 4718596
Sparse Core Ops, SparseCore 0:
  11.1 72.4 all-gather.2

commit v4 on v3

--- a/solution.py
+++ b/solution.py
@@ -136,7 +136,7 @@
 
 
 def key_value_kernel(w_ref, *refs):
-    rows_refs, (pair_ref, state_ref, sent_ref) = refs[:GROUP], refs[GROUP:]
+    rows_refs, (pair_ref, sent_ref) = refs[:GROUP], refs[GROUP:]
     own_width = w_ref.shape[1] // 2
     for j, x_ref in enumerate(rows_refs):
 
@@ -155,7 +155,6 @@
                     (((0,), (0,)), ((), ())),
                     preferred_element_type=jnp.float32,
                 )
-                state_ref[0, h] = state
                 sent_ref[0, h] = state.astype(jnp.bfloat16)
 
 
@@ -164,10 +163,9 @@
     columns = weight.shape[1]
     heads = columns // 2 // HD
     pair = out_like((GROUP, rows, columns), jnp.bfloat16)
-    state = out_like((GROUP, heads, HD, HD), jnp.float32)
     sent = out_like((GROUP, heads, HD, HD), jnp.bfloat16)
     inputs = [weight, *everyone]
-    outputs = [pair, state, sent]
+    outputs = [pair, sent]
     flops = 2 * GROUP * rows * width * columns
     return call(
         key_value_kernel, "keys_values_states", GROUP, inputs, [whole(a) for a in inputs],
@@ -323,7 +321,7 @@
 
 def expert_rows(rows, inner_weight, outer_weight):
     count, width = rows.shape
-    chunks, inner, outer = FF // 256, 256, 512
+    chunks, inner, outer = FF // 512, 512, 1024
     last = chunks - 1
     inputs = [rows, inner_weight, inner_weight, outer_weight]
     output = out_like((count, width), jnp.bfloat16)
@@ -367,9 +365,9 @@
     first, prior, send, weigh = lax.optimization_barrier((first, tuple(prior), send, weigh))
     prior = jnp.stack(prior)
 
-    pair, state, sent = keys_values_states(first.reshape(width, 2 * own_width), everyone)
+    pair, sent = keys_values_states(first.reshape(width, 2 * own_width), everyone)
     in_row = [shift_ctx(sent, 0, d).astype(jnp.float32) for d in range(1, SIDE)]
-    total = (state + in_row[0] + in_row[1] + in_row[2]).astype(jnp.bfloat16)
+    total = (sent.astype(jnp.float32) + in_row[0] + in_row[1] + in_row[2]).astype(jnp.bfloat16)
     base = prior
     for d in range(1, SIDE):
         base = base + jnp.where(row >= d, in_row[d - 1], 0.0)

time: 310 us -> 310 us (level)
  no operation moved by 1% of the time
where the time goes in v4:
time: 310 us; the launch traced here: 304 us
  blocking collectives  153 us (49%)
  waiting for transfers between devices  51.4 us (17%)
  Pallas kernels  46.8 us (15%)
  starting transfers between devices  20 us (6%)
  between operations  13.6 us (4%)
  other arithmetic  7.87 us (3%)
  local copies, waits for them, and re-layouts  7.31 us (2%)
  matrix products  3.65 us (1%)
    all_to_all x1, blocking collectives, shards(): lax.all_to_all(outgoing, 'ctx', split_axis=0, concat_axis=0, tiled=True)  77.4 us
    all_to_all x1, blocking collectives, shards(): lax.all_to_all(result.reshape(experts, capacity, width), 'ctx', split_axi...  75.7 us
    pallas_call x6, Pallas kernels, call(): pl.pallas_call(kernel, grid=(grid,), in_specs=in_specs, out_specs=out_spe...  46.8 us
    ppermute x10, waiting for transfers between devices, swap_with(): lax.ppermute(x, 'dp', [(i, i ^ mask) for i in range(lax.axis_size('dp'))])  26.5 us
    ppermute x6, waiting for transfers between devices, shift_ctx(): return lax.ppermute(x, 'ctx', pairs)  23.2 us
    ppermute x6, starting transfers between devices, shift_ctx(): return lax.ppermute(x, 'ctx', pairs)  8.12 us
    all_to_all x1, starting transfers between devices, shards(): lax.all_to_all(spread, 'ctx', split_axis=0, concat_axis=0, tiled=True)  7.24 us
  transfers between devices with their start and end apart: 18, of which 10 were waited for; matrix products, arithmetic and copies ran while one was open for 3% of the time, Pallas kernels for 5%

profile of v4, /device:TPU:124, one launch (start us, length us, event | category | flops | bytes accessed | tf_op | source)
XLA Modules:
  0.0 303.8 jit_solution(5568969794077336624)
XLA Ops:
  6.5 4.4 %prepared.1 = (bf16[16,128,512]{2,1,0:T(8,128)(2,1)}, bf16[384,256]{1,0:T(8,128)(2,1)}, bf16[256,2048]{1,0:T(8,128)(2,1)}) custom-call(s32[1]{0:T(128)} %bitcast.where_ref, bf16[256,2048]{1,0:T(8,128)(2,1)} %tokens_ref.3, bf16[128,3072]{1,0:T(8,128)(2,1)} %qkv_ref.1, bf16[64,2048]{1,0:T(8,128)(2,1)} %out_ref.1), custom_call_target="tpu_custom_call" | custom-call | flops 2097152 | bytes 5439492 | tf_op jit(solution)/shard_map/prepared/pallas_call | solution.py:75
  11.5 7.2 %all-to-all-start = ((bf16[16,128,512]{2,1,0:T(8,128)(2,1)}), bf16[16,128,512]{2,1,0:T(8,128)(2,1)S(1)}, u32[]{:S(2)}, u32[]{:S(2)}) async-start(bf16[16,128,512]{2,1,0:T(8,128)(2,1)} %get-tuple-element.28), calls=%async_computation | async-start | bytes 4194304 | tf_op jit(solution)/shard_map/all_to_all | solution.py:359
  18.8 17.4 %collective-permute-done.4.refs_2_ = bf16[256,2048]{1,0:T(8,128)(2,1)} collective-permute-done((bf16[256,2048]{1,0:T(8,128)(2,1)}, bf16[256,2048]{1,0:T(8,128)(2,1)}, u32[]{:S(2)}, u32[]{:S(2)}) %collective-permute-start.4) | collective-permute-done | bytes 1048608 | tf_op jit(solution)/shard_map/ppermute | solution.py:24
  36.3 1.8 constant_dynamic-slice_fusion
  38.7 1.6 collective-permute-start.1
  42.3 1.3 pad_maximum_fusion
  43.6 1.1 fusion.4.send_ref
  44.7 2.3 collective-permute-done.1
  47.1 1.0 all-to-all-done
  48.1 5.7 %keys_values_states.1 = (bf16[4,256,512]{2,1,0:T(8,128)(2,1)S(1)}, bf16[4,2,128,128]{3,2,1,0:T(8,128)(2,1)S(1)}) custom-call(bf16[2048,512]{1,0:T(8,128)(2,1)S(1)} %bitcast.47, bf16[256,2048]{1,0:T(8,128)(2,1)S(1)} %copy-done.5, bf16[256,2048]{1,0:T(8,128)(2,1)} %collective-permute-done.3.refs_1_, bf16[256,2048]{1,0:T(8,128)(2,1)} %collective-permute-done.4.refs_2_, ...), custom_call_target="tpu_custom_call" | custom-call | flops 2147483648 | bytes 7602176 | tf_op jit(solution)/shard_map/keys_values_states/pallas_call | solution.py:75
  54.8 1.2 collective-permute-start.8
  56.0 2.5 collective-permute-start.7
  58.5 1.2 collective-permute-start.6
  59.6 12.5 %collective-permute-done.8 = bf16[4,2,128,128]{3,2,1,0:T(8,128)(2,1)S(1)} collective-permute-done((bf16[4,2,128,128]{3,2,1,0:T(8,128)(2,1)S(1)}, bf16[4,2,128,128]{3,2,1,0:T(8,128)(2,1)S(1)}, u32[]{:S(2)}, u32[]{:S(2)}) %collective-permute-start.8) | collective-permute-done | bytes 262176 | tf_op jit(solution)/shard_map/ppermute | solution.py:33
  72.2 5.2 %collective-permute-done.7 = bf16[4,2,128,128]{3,2,1,0:T(8,128)(2,1)S(1)} collective-permute-done((bf16[4,2,128,128]{3,2,1,0:T(8,128)(2,1)S(1)}, bf16[4,2,128,128]{3,2,1,0:T(8,128)(2,1)S(1)}, u32[]{:S(2)}, u32[]{:S(2)}) %collective-permute-start.7) | collective-permute-done | bytes 262176 | tf_op jit(solution)/shard_map/ppermute | solution.py:33
  77.3 2.7 collective-permute-done.6
  80.1 2.2 fusion.8
  83.4 2.7 collective-permute-start.10
  86.2 1.9 copy-done
  88.0 1.2 copy-done.6
  89.3 1.2 copy-done.8
  90.5 6.0 %queries_inside.1 = (bf16[4,256,256]{2,1,0:T(8,128)(2,1)S(1)}, f32[4,256,256]{2,1,0:T(8,128)S(1)}) custom-call(bf16[16,384,256]{2,1,0:T(8,128)(2,1)S(1)} %bitcast.41, bf16[4,256,512]{2,1,0:T(8,128)(2,1)S(1)} %copy-done.8, bf16[256,2048]{1,0:T(8,128)(2,1)S(1)} %copy-done.6, bf16[256,2048]{1,0:T(8,128)(2,1)} %collective-permute-done.3.refs_1_, ...), custom_call_target="tpu_custom_call" | custom-call | flops 1342177280 | bytes 9961472 | tf_op jit(solution)/shard_map/queries_inside/pallas_call | solution.py:75
  96.5 2.8 collective-permute-done.9.refs_0_
  99.3 3.1 %finished_heads.1 = bf16[4,256,256]{2,1,0:T(8,128)(2,1)S(1)} custom-call(s32[1]{0:T(128)} %bitcast.6.where_ref, bf16[4,256,256]{2,1,0:T(8,128)(2,1)S(1)} %get-tuple-element.36.query_ref, f32[4,256,256]{2,1,0:T(8,128)S(1)} %get-tuple-element.37.inside_ref, f32[4,2,128,128]{3,2,1,0:T(8,128)S(1)} %copy-done.4, ...), custom_call_target="tpu_custom_call" | custom-call | flops 134217728 | bytes 3407876 | tf_op jit(solution)/shard_map/finished_heads/pallas_call | solution.py:75
  104.4 3.7 %collective-permute-done.14.refs_3_ = bf16[256,256]{1,0:T(8,128)(2,1)S(1)} collective-permute-done((bf16[256,256]{1,0:T(8,128)(2,1)S(1)}, bf16[256,256]{1,0:T(8,128)(2,1)S(1)}, u32[]{:S(2)}, u32[]{:S(2)}) %collective-permute-start.14) | collective-permute-done | bytes 131104 | tf_op jit(solution)/shard_map/ppermute | solution.py:24
  108.1 3.0 collective-permute-done.13.refs_2_
  111.2 4.5 %projected_rows.1 = (bf16[256,2048]{1,0:T(8,128)(2,1)S(1)}, bf16[1536,2048]{1,0:T(8,128)(2,1)S(1)}) custom-call(s32[1]{0:T(128)} %bitcast.where_ref, bf16[256,2048]{1,0:T(8,128)(2,1)S(1)} %copy-done.2, bf16[1536,256]{1,0:T(8,128)(2,1)S(1)} %copy-done.3, bf16[256,256]{1,0:T(8,128)(2,1)S(1)} %get-tuple-element.58.refs_0_, ...), custom_call_target="tpu_custom_call" | custom-call | flops 2684354560 | bytes 22282244 | tf_op jit(solution)/shard_map/projected_rows/pallas_call | solution.py:75
  115.6 77.4 %all_to_all.15 = bf16[16,96,2048]{2,1,0:T(8,128)(2,1)S(1)} all-to-all(bf16[16,96,2048]{2,1,0:T(8,128)(2,1)S(1)} %bitcast.44), channel_id=1, replica_groups=mesh['dp'=8,'ctx'=16] {'ctx'}, dimensions={0} | all-to-all | bytes 12582912 | tf_op jit(solution)/shard_map/all_to_all | solution.py:386
  193.0 23.2 %expert_rows.1 = bf16[1536,2048]{1,0:T(8,128)(2,1)S(1)} custom-call(bf16[1536,2048]{1,0:T(8,128)(2,1)S(1)} %bitcast.45, bf16[2048,2048]{1,0:T(8,128)(2,1)} %bitcast.54, bf16[2048,2048]{1,0:T(8,128)(2,1)} %bitcast.55, bf16[1024,2048]{1,0:T(8,128)(2,1)S(1)} %bitcast.48), custom_call_target="tpu_custom_call" | custom-call | flops 19327352832 | bytes 33554432 | tf_op jit(solution)/shard_map/expert_rows/pallas_call | solution.py:75
  216.2 75.7 %all_to_all.16 = bf16[16,96,2048]{2,1,0:T(8,128)(2,1)S(1)} all-to-all(bf16[16,96,2048]{2,1,0:T(8,128)(2,1)S(1)} %bitcast.46), channel_id=1, replica_groups=mesh['dp'=8,'ctx'=16] {'ctx'}, dimensions={0} | all-to-all | bytes 12582912 | tf_op jit(solution)/shard_map/all_to_all | solution.py:390
  291.9 3.5 %fusion.11 = f32[512,2048]{1,0:T(8,128)S(1)} fusion(bf16[512,1536]{0,1:T(8,128)(2,1)S(1)} %copy-done.10, bf16[1536,2048]{1,0:T(8,128)(2,1)S(1)} %bitcast.49), kind=kOutput, calls=%fused_computation.34 | convolution fusion | flops 3221225472 | bytes 12058624 | tf_op jit(solution)/shard_map/dot_general | solution.py:393
  295.4 1.5 fusion.1
  (53 shorter events, 7.3 us)
Async XLA Ops:
  6.5 76.3 %all-gather.3.cloned.1.call-start = ((), (), s32[]{:S(2)}) async-start(), calls=%async_computation.3 | async-start | bytes 3342336 | tf_op jit(solution)/shard_map/all_gather | solution.py:356
  11.0 25.3 %collective-permute-start.4 = (bf16[256,2048]{1,0:T(8,128)(2,1)}, bf16[256,2048]{1,0:T(8,128)(2,1)}, u32[]{:S(2)}, u32[]{:S(2)}) collective-permute-start(bf16[256,2048]{1,0:T(8,128)(2,1)} %get-tuple-element.32.refs_0_), channel_id=1, source_target_pairs={{0,32},{16,48},{32,0},{48,16},{64,96},{80,112},{96,64},{112,80},{1... | collective-permute-start | bytes 3145736 | tf_op jit(solution)/shard_map/ppermute | solution.py:24
  11.5 7.2 %copy-start.5 = (bf16[256,2048]{1,0:T(8,128)(2,1)S(1)}, bf16[256,2048]{1,0:T(8,128)(2,1)}, u32[]{:S(2)}) copy-start(bf16[256,2048]{1,0:T(8,128)(2,1)} %get-tuple-element.32.refs_0_) | copy-start | bytes 3145732
  11.5 36.6 %all-to-all-start = ((bf16[16,128,512]{2,1,0:T(8,128)(2,1)}), bf16[16,128,512]{2,1,0:T(8,128)(2,1)S(1)}, u32[]{:S(2)}, u32[]{:S(2)}) async-start(bf16[16,128,512]{2,1,0:T(8,128)(2,1)} %get-tuple-element.28), calls=%async_computation | async-start | bytes 4194304 | tf_op jit(solution)/shard_map/all_to_all | solution.py:359
  18.7 29.3 %collective-permute-start.3 = (bf16[256,2048]{1,0:T(8,128)(2,1)S(1)}, bf16[256,2048]{1,0:T(8,128)(2,1)}, u32[]{:S(2)}, u32[]{:S(2)}) collective-permute-start(bf16[256,2048]{1,0:T(8,128)(2,1)S(1)} %copy-done.5), channel_id=1, source_target_pairs={{0,16},{16,0},{32,48},{48,32},{64,80},{80,64},{96,112},{112,96},{1... | collective-permute-start | bytes 3145736 | tf_op jit(solution)/shard_map/ppermute | solution.py:24
  36.3 11.8 %collective-permute-start.5 = (bf16[256,2048]{1,0:T(8,128)(2,1)}, bf16[256,2048]{1,0:T(8,128)(2,1)}, u32[]{:S(2)}, u32[]{:S(2)}) collective-permute-start(bf16[256,2048]{1,0:T(8,128)(2,1)} %collective-permute-done.4.refs_2_), channel_id=1, source_target_pairs={{0,16},{16,0},{32,48},{48,32},{64,80},{80,64},{96,112},{112,96},{1... | collective-permute-start | bytes 3145736 | tf_op jit(solution)/shard_map/ppermute | solution.py:24
  38.1 6.6 %collective-permute-start.2 = (f32[2,128,128]{2,1,0:T(8,128)}, f32[2,128,128]{2,1,0:T(8,128)S(1)}, u32[]{:S(2)}, u32[]{:S(2)}) collective-permute-start(f32[2,128,128]{2,1,0:T(8,128)} %get-tuple-element.59), channel_id=1, source_target_pairs={{0,48},{16,32},{32,16},{48,0},{64,112},{80,96},{96,80},{112,64},{1... | collective-permute-start | bytes 393224 | tf_op jit(solution)/shard_map/ppermute | solution.py:24
  38.6 6.1 %collective-permute-start = (f32[2,128,128]{2,1,0:T(8,128)}, f32[2,128,128]{2,1,0:T(8,128)S(1)}, u32[]{:S(2)}, u32[]{:S(2)}) collective-permute-start(f32[2,128,128]{2,1,0:T(8,128)} %get-tuple-element.60), channel_id=1, source_target_pairs={{0,16},{16,0},{32,48},{48,32},{64,80},{80,64},{96,112},{112,96},{1... | collective-permute-start | bytes 393224 | tf_op jit(solution)/shard_map/ppermute | solution.py:24
  38.7 8.4 %collective-permute-start.1 = (f32[2,128,128]{2,1,0:T(8,128)}, f32[2,128,128]{2,1,0:T(8,128)}, u32[]{:S(2)}, u32[]{:S(2)}) collective-permute-start(f32[2,128,128]{2,1,0:T(8,128)} %get-tuple-element.62), channel_id=1, source_target_pairs={{0,32},{16,48},{32,0},{48,16},{64,96},{80,112},{96,64},{112,80},{1... | collective-permute-start | bytes 393224 | tf_op jit(solution)/shard_map/ppermute | solution.py:24
  44.7 3.3 %copy-start.11 = (f32[2,128,128]{2,1,0:T(8,128)}, f32[2,128,128]{2,1,0:T(8,128)S(1)}, u32[]{:S(2)}) copy-start(f32[2,128,128]{2,1,0:T(8,128)S(1)} %collective-permute-done.2) | copy-start | bytes 393220
  44.7 3.3 %copy-start.12 = (f32[2,128,128]{2,1,0:T(8,128)}, f32[2,128,128]{2,1,0:T(8,128)S(1)}, u32[]{:S(2)}) copy-start(f32[2,128,128]{2,1,0:T(8,128)S(1)} %collective-permute-done) | copy-start | bytes 393220
  53.8 1.0 copy-start.7
  54.8 17.4 %collective-permute-start.8 = (bf16[4,2,128,128]{3,2,1,0:T(8,128)(2,1)S(1)}, bf16[4,2,128,128]{3,2,1,0:T(8,128)(2,1)S(1)}, u32[]{:S(2)}, u32[]{:S(2)}) collective-permute-start(bf16[4,2,128,128]{3,2,1,0:T(8,128)(2,1)S(1)} %get-tuple-element.33), channel_id=1, source_target_pairs={{0,3},{1,0},{2,1},{3,2},{4,7},{5,4},{6,5},{7,6},{8,11},{9,8},{10,9... | collective-permute-start | bytes 786440 | tf_op jit(solution)/shard_map/ppermute | solution.py:33
  56.0 21.4 %collective-permute-start.7 = (bf16[4,2,128,128]{3,2,1,0:T(8,128)(2,1)S(1)}, bf16[4,2,128,128]{3,2,1,0:T(8,128)(2,1)S(1)}, u32[]{:S(2)}, u32[]{:S(2)}) collective-permute-start(bf16[4,2,128,128]{3,2,1,0:T(8,128)(2,1)S(1)} %get-tuple-element.33), channel_id=1, source_target_pairs={{0,2},{1,3},{2,0},{3,1},{4,6},{5,7},{6,4},{7,5},{8,10},{9,11},{10,... | collective-permute-start | bytes 786440 | tf_op jit(solution)/shard_map/ppermute | solution.py:33
  58.5 21.6 %collective-permute-start.6 = (bf16[4,2,128,128]{3,2,1,0:T(8,128)(2,1)S(1)}, bf16[4,2,128,128]{3,2,1,0:T(8,128)(2,1)S(1)}, u32[]{:S(2)}, u32[]{:S(2)}) collective-permute-start(bf16[4,2,128,128]{3,2,1,0:T(8,128)(2,1)S(1)} %get-tuple-element.33), channel_id=1, source_target_pairs={{0,1},{1,2},{2,3},{3,0},{4,5},{5,6},{6,7},{7,4},{8,9},{9,10},{10,1... | collective-permute-start | bytes 786440 | tf_op jit(solution)/shard_map/ppermute | solution.py:33
  82.9 28.3 %collective-permute-start.15 = (bf16[16,384,256]{2,1,0:T(8,128)(2,1)}, bf16[16,384,256]{2,1,0:T(8,128)(2,1)S(1)}, u32[]{:S(2)}, u32[]{:S(2)}) collective-permute-start(bf16[16,384,256]{2,1,0:T(8,128)(2,1)} %bitcast.40), channel_id=1, source_target_pairs={{0,16},{16,0},{32,48},{48,32},{64,80},{80,64},{96,112},{112,96},{1... | collective-permute-start | bytes 9437192 | tf_op jit(solution)/shard_map/ppermute | solution.py:24
  82.9 13.6 %collective-permute-start.11 = (bf16[4,2,128,128]{3,2,1,0:T(8,128)(2,1)}, bf16[4,2,128,128]{3,2,1,0:T(8,128)(2,1)S(1)}, u32[]{:S(2)}, u32[]{:S(2)}) collective-permute-start(bf16[4,2,128,128]{3,2,1,0:T(8,128)(2,1)} %get-tuple-element.54), channel_id=1, source_target_pairs={{0,12},{1,13},{2,14},{3,15},{4,0},{5,1},{6,2},{7,3},{8,4},{9,5},{1... | collective-permute-start | bytes 786440 | tf_op jit(solution)/shard_map/ppermute | solution.py:33
  83.4 13.1 %collective-permute-start.10 = (bf16[4,2,128,128]{3,2,1,0:T(8,128)(2,1)}, bf16[4,2,128,128]{3,2,1,0:T(8,128)(2,1)}, u32[]{:S(2)}, u32[]{:S(2)}) collective-permute-start(bf16[4,2,128,128]{3,2,1,0:T(8,128)(2,1)} %get-tuple-element.54), channel_id=1, source_target_pairs={{0,8},{1,9},{2,10},{3,11},{4,12},{5,13},{6,14},{7,15},{8,0},{9,1},... | collective-permute-start | bytes 786440 | tf_op jit(solution)/shard_map/ppermute | solution.py:33
  86.2 13.1 %collective-permute-start.9 = (bf16[4,2,128,128]{3,2,1,0:T(8,128)(2,1)}, bf16[4,2,128,128]{3,2,1,0:T(8,128)(2,1)}, u32[]{:S(2)}, u32[]{:S(2)}) collective-permute-start(bf16[4,2,128,128]{3,2,1,0:T(8,128)(2,1)} %get-tuple-element.54), channel_id=1, source_target_pairs={{0,4},{1,5},{2,6},{3,7},{4,8},{5,9},{6,10},{7,11},{8,12},{9,13},{1... | collective-permute-start | bytes 786440 | tf_op jit(solution)/shard_map/ppermute | solution.py:33
  86.2 1.9 copy-start
  88.0 1.2 copy-start.6
  89.3 1.2 copy-start.8
  90.5 8.8 %copy-start.4 = (f32[4,2,128,128]{3,2,1,0:T(8,128)S(1)}, f32[4,2,128,128]{3,2,1,0:T(8,128)}, u32[]{:S(2)}) copy-start(f32[4,2,128,128]{3,2,1,0:T(8,128)} %get-tuple-element.53.base_ref) | copy-start | bytes 1572868
  90.5 20.6 %copy-start.3 = (bf16[1536,256]{1,0:T(8,128)(2,1)S(1)}, bf16[1536,256]{1,0:T(8,128)(2,1)}, u32[]{:S(2)}) copy-start(bf16[1536,256]{1,0:T(8,128)(2,1)} %fusion.4.send_ref) | copy-start | bytes 2359300
  99.3 11.8 %copy-start.1 = (bf16[6144,256]{1,0:T(8,128)(2,1)S(1)}, bf16[6144,256]{1,0:T(8,128)(2,1)}, u32[]{:S(2)}) copy-start(bf16[6144,256]{1,0:T(8,128)(2,1)} %all-gather.3.cloned.1.call-done) | copy-start | bytes 9437188
  99.3 11.9 %copy-start.2 = (bf16[256,2048]{1,0:T(8,128)(2,1)S(1)}, bf16[256,2048]{1,0:T(8,128)(2,1)}, u32[]{:S(2)}) copy-start(bf16[256,2048]{1,0:T(8,128)(2,1)} %tokens_ref.3) | copy-start | bytes 3145732
  102.4 5.7 %collective-permute-start.14 = (bf16[256,256]{1,0:T(8,128)(2,1)S(1)}, bf16[256,256]{1,0:T(8,128)(2,1)S(1)}, u32[]{:S(2)}, u32[]{:S(2)}) collective-permute-start(bf16[256,256]{1,0:T(8,128)(2,1)S(1)} %get-tuple-element.55), channel_id=1, source_target_pairs={{0,48},{16,32},{32,16},{48,0},{64,112},{80,96},{96,80},{112,64},{1... | collective-permute-start | bytes 393224 | tf_op jit(solution)/shard_map/ppermute | solution.py:24
  103.2 7.9 %collective-permute-start.13 = (bf16[256,256]{1,0:T(8,128)(2,1)S(1)}, bf16[256,256]{1,0:T(8,128)(2,1)S(1)}, u32[]{:S(2)}, u32[]{:S(2)}) collective-permute-start(bf16[256,256]{1,0:T(8,128)(2,1)S(1)} %get-tuple-element.56), channel_id=1, source_target_pairs={{0,32},{16,48},{32,0},{48,16},{64,96},{80,112},{96,64},{112,80},{1... | collective-permute-start | bytes 393224 | tf_op jit(solution)/shard_map/ppermute | solution.py:24
  104.2 7.0 %collective-permute-start.12 = (bf16[256,256]{1,0:T(8,128)(2,1)S(1)}, bf16[256,256]{1,0:T(8,128)(2,1)S(1)}, u32[]{:S(2)}, u32[]{:S(2)}) collective-permute-start(bf16[256,256]{1,0:T(8,128)(2,1)S(1)} %get-tuple-element.57), channel_id=1, source_target_pairs={{0,16},{16,0},{32,48},{48,32},{64,80},{80,64},{96,112},{112,96},{1... | collective-permute-start | bytes 393224 | tf_op jit(solution)/shard_map/ppermute | solution.py:24
  115.6 77.4 %copy-start.9 = (bf16[1,1024,2048]{2,1,0:T(8,128)(2,1)S(1)}, bf16[1,1024,2048]{2,1,0:T(8,128)(2,1)}, u32[]{:S(2)}) copy-start(bf16[1,1024,2048]{2,1,0:T(8,128)(2,1)} %param.15) | copy-start | bytes 12582916
  216.2 75.7 %copy-start.10 = (bf16[512,1536]{0,1:T(8,128)(2,1)S(1)}, bf16[512,1536]{0,1:T(8,128)(2,1)}, u32[]{:S(2)}) copy-start(bf16[512,1536]{0,1:T(8,128)(2,1)} %pad_maximum_fusion) | copy-start | bytes 4718596
Sparse Core Ops, SparseCore 0:
  11.1 71.7 all-gather.2
